TPU v7x, 256 devices: a whole 4x4x8 slice. The times are simulated.
256 devices in a mesh: section: 8 (over x, core), span: 32 (over y, z).
Axes of the slice: x: 4, y: 4, z: 8, core: 2. Of those that a mesh axis runs over, the one named last changes fastest.
Arguments:
- inverse_blocks: bfloat16 [32, 768, 768], P('section'), may hold values from -1.2 to 1.2
- coupling: float32 [32, 768], P('section'), may hold values from 0.05 to 0.3
- sources: bfloat16 [8, 768, 12288], P('section', None, 'span'), may hold values from -36 to 36
Outputs:
- basis: bfloat16 [8, 768, 12288], P('section', None, 'span')
- upper: float32 [8, 48, 48], P('section')
All inputs are finite; a program needn't handle non-finite values.
Results may differ from a plain program's by a relative error of at most 0.03.
Values may be sent and summed in bfloat16 or wider, within the bound.
A program may use at most 64 MiB of HBM per device.

v0:
```python
import jax
import jax.numpy as jnp
from jax import lax
from jax.sharding import PartitionSpec as P

K = 48
STATIONS = 4
FN = 768


def padded(block, sides, width):
    for axis, dim in sides:
        count = lax.axis_size(axis)
        forward = [(i, i + 1) for i in range(count - 1)]
        forward.append((count - 1, 0))
        backward = [(target, source) for source, target in forward]
        low = lax.ppermute(
            lax.slice_in_dim(block, block.shape[dim] - width, None, axis=dim), axis, forward
        )
        high = lax.ppermute(lax.slice_in_dim(block, 0, width, axis=dim), axis, backward)
        block = jnp.concatenate([low, block, high], axis=dim)
    return block


def from_behind(value, axis, by):
    devices = lax.axis_size(axis)
    pairs = [(i, i + by) for i in range(devices) if 0 <= i + by < devices]
    return lax.ppermute(value, axis, pairs)


def apply_station(extended, blocks, rates):
    wide = extended.astype(jnp.float32)
    center = wide[:, 1:-1]
    spread = wide[:, 2:] + wide[:, :-2] - 2.0 * center
    update = (center + rates[:, None, None] * spread).astype(jnp.bfloat16)
    moved = jnp.dot(blocks, update.reshape(blocks.shape[0], -1), preferred_element_type=jnp.float32)
    return moved.astype(jnp.bfloat16).reshape(update.shape)


def march_block(state, inverse_blocks, coupling):
    for station in reversed(range(STATIONS)):
        extended = padded(state, (("span", 1),), 1)
        state = apply_station(extended, inverse_blocks[station], coupling[station])
    return state


def local(inverse_blocks, coupling, sources):
    local_span = sources.shape[2] // K
    sections = lax.axis_size("section")
    span_count = lax.axis_size("span")
    group_index = lax.axis_index("section")
    pieces = 1
    block_cols = K // pieces
    source_all = sources[0].reshape(FN, local_span, K)

    def one_round(round_index, state_pair):
        incoming, result = state_pair
        block_number = round_index - (sections - 1 - group_index)
        active = jnp.logical_and(block_number >= 0, block_number < pieces)
        added = incoming.astype(jnp.float32) + source_all.astype(jnp.float32)
        state = march_block(added.astype(jnp.bfloat16), inverse_blocks, coupling)
        result = jnp.where(active, state, result)
        incoming = from_behind(state, "section", -1)
        return (incoming, result)

    start_pair = (
        jnp.zeros((FN, local_span, block_cols), jnp.bfloat16),
        jnp.zeros((FN, local_span, K), jnp.bfloat16),
    )
    final_pair = lax.fori_loop(0, sections + pieces - 1, one_round, start_pair)
    inlet = final_pair[1]
    flat_rows = inlet.reshape(FN * local_span, K)
    partial_gram = jnp.dot(flat_rows.T, flat_rows, preferred_element_type=jnp.float32)
    summed = lax.psum(partial_gram, "span")
    scaled = summed / float(FN * local_span * span_count)
    factor = jnp.linalg.cholesky(scaled)
    inverse = jax.scipy.linalg.solve_triangular(factor, jnp.eye(K, dtype=jnp.float32), lower=True)
    basis_rows = jnp.dot(flat_rows.astype(jnp.float32), inverse.T, precision=lax.Precision.HIGHEST)
    basis_local = basis_rows.astype(jnp.bfloat16).reshape(1, FN, local_span * K)
    return (basis_local, factor.T[None])


def solution(mesh):
    placed = (P("section", None, None), P("section", None), P("section", None, "span"))
    return jax.shard_map(
        local,
        mesh=mesh,
        in_specs=placed,
        out_specs=(P("section", None, "span"), P("section", None, None)),
        check_vma=False,
    )
```

profile of v0, /device:TPU:2, one launch (start us, length us, event | category | flops | bytes accessed | tf_op | source)
XLA Modules:
  0.0 543.8 jit_solution(8101770290278956013)
XLA Ops:
  2.0 387.8 %while.18 = (s32[]{:T(128)}, bf16[768,8,48]{0,2,1:T(8,128)(2,1)S(1)}, bf16[768,8,48]{0,2,1:T(8,128)(2,1)S(1)}, bf16[768,8,48]{0,2,1:T(8,128)(2,1)S(1)}, f32[4,76...) while((s32[]{:T(128)}, ...), condition=%wide.region_1.2_spmd.clone, body=%wide.region_0.1_spmd.clone.sunk | while | flops 1826390016 | bytes 63148552 | solution.py:70
  2.2 8.4 %collective-permute-start = (bf16[768,1,48]{0,2,1:T(8,128)(2,1)S(1)}, bf16[768,1,48]{0,2,1:T(8,128)(2,1)S(1)}, u32[]{:S(2)}, u32[]{:S(2)}) collective-permute-start(bf16[768,1,48]{0,2,1:T(8,128)(2,1)S(1)} %get-tuple-element.284), channel_id=1, source_target_pairs={{1,0},{2,1},{3,2},{4,3},{5,4},{6,5},{7,6},{8,7},{9,8},{10,9},{11,1... | collective-permute-start | bytes 221192 | tf_op jit(solution)/shard_map/while/body/eval_jaxpr/ppermute | solution.py:20
  12.6 5.7 %collective-permute-done.1 = bf16[768,1,48]{0,2,1:T(8,128)(2,1)S(1)} collective-permute-done((bf16[768,1,48]{0,2,1:T(8,128)(2,1)S(1)}, bf16[768,1,48]{0,2,1:T(8,128)(2,1)S(1)}, u32[]{:S(2)}, u32[]{:S(2)}) %collective-permute-start.1) | collective-permute-done | bytes 73760 | tf_op jit(solution)/shard_map/while/body/eval_jaxpr/ppermute | solution.py:17
  25.7 3.4 collective-permute-done.3
  34.6 3.4 collective-permute-done.5
  43.5 3.4 collective-permute-done.7
  50.1 7.1 %collective-permute-done.8 = bf16[768,8,48]{0,2,1:T(8,128)(2,1)S(1)} collective-permute-done((bf16[768,8,48]{0,2,1:T(8,128)(2,1)S(1)}, bf16[768,8,48]{0,2,1:T(8,128)(2,1)S(1)}, u32[]{:S(2)}, u32[]{:S(2)}) %collective-permute-start.8) | collective-permute-done | bytes 589856 | tf_op jit(solution)/shard_map/while/body/eval_jaxpr/ppermute | solution.py:28
  61.8 3.4 collective-permute-done.1
  70.4 2.8 collective-permute-done.2
  73.1 3.4 collective-permute-done.3
  82.0 3.5 collective-permute-done.5
  91.0 3.4 collective-permute-done.7
  97.6 7.1 %collective-permute-done.8 = bf16[768,8,48]{0,2,1:T(8,128)(2,1)S(1)} collective-permute-done((bf16[768,8,48]{0,2,1:T(8,128)(2,1)S(1)}, bf16[768,8,48]{0,2,1:T(8,128)(2,1)S(1)}, u32[]{:S(2)}, u32[]{:S(2)}) %collective-permute-start.8) | collective-permute-done | bytes 589856 | tf_op jit(solution)/shard_map/while/body/eval_jaxpr/ppermute | solution.py:28
  109.3 3.4 collective-permute-done.1
  117.9 2.8 collective-permute-done.2
  120.7 3.4 collective-permute-done.3
  129.5 3.5 collective-permute-done.5
  138.5 3.4 collective-permute-done.7
  145.1 7.1 %collective-permute-done.8 = bf16[768,8,48]{0,2,1:T(8,128)(2,1)S(1)} collective-permute-done((bf16[768,8,48]{0,2,1:T(8,128)(2,1)S(1)}, bf16[768,8,48]{0,2,1:T(8,128)(2,1)S(1)}, u32[]{:S(2)}, u32[]{:S(2)}) %collective-permute-start.8) | collective-permute-done | bytes 589856 | tf_op jit(solution)/shard_map/while/body/eval_jaxpr/ppermute | solution.py:28
  156.9 3.4 collective-permute-done.1
  165.4 2.8 collective-permute-done.2
  168.2 3.4 collective-permute-done.3
  177.0 3.5 collective-permute-done.5
  186.0 3.4 collective-permute-done.7
  192.6 7.1 %collective-permute-done.8 = bf16[768,8,48]{0,2,1:T(8,128)(2,1)S(1)} collective-permute-done((bf16[768,8,48]{0,2,1:T(8,128)(2,1)S(1)}, bf16[768,8,48]{0,2,1:T(8,128)(2,1)S(1)}, u32[]{:S(2)}, u32[]{:S(2)}) %collective-permute-start.8) | collective-permute-done | bytes 589856 | tf_op jit(solution)/shard_map/while/body/eval_jaxpr/ppermute | solution.py:28
  204.4 3.4 collective-permute-done.1
  215.7 3.4 collective-permute-done.3
  224.6 3.5 collective-permute-done.5
  233.5 3.4 collective-permute-done.7
  240.1 7.1 %collective-permute-done.8 = bf16[768,8,48]{0,2,1:T(8,128)(2,1)S(1)} collective-permute-done((bf16[768,8,48]{0,2,1:T(8,128)(2,1)S(1)}, bf16[768,8,48]{0,2,1:T(8,128)(2,1)S(1)}, u32[]{:S(2)}, u32[]{:S(2)}) %collective-permute-start.8) | collective-permute-done | bytes 589856 | tf_op jit(solution)/shard_map/while/body/eval_jaxpr/ppermute | solution.py:28
  251.9 3.4 collective-permute-done.1
  263.2 3.4 collective-permute-done.3
  272.1 3.5 collective-permute-done.5
  281.0 3.4 collective-permute-done.7
  287.7 7.1 %collective-permute-done.8 = bf16[768,8,48]{0,2,1:T(8,128)(2,1)S(1)} collective-permute-done((bf16[768,8,48]{0,2,1:T(8,128)(2,1)S(1)}, bf16[768,8,48]{0,2,1:T(8,128)(2,1)S(1)}, u32[]{:S(2)}, u32[]{:S(2)}) %collective-permute-start.8) | collective-permute-done | bytes 589856 | tf_op jit(solution)/shard_map/while/body/eval_jaxpr/ppermute | solution.py:28
  299.4 3.4 collective-permute-done.1
  310.7 3.4 collective-permute-done.3
  319.6 3.5 collective-permute-done.5
  328.6 3.4 collective-permute-done.7
  335.2 7.1 %collective-permute-done.8 = bf16[768,8,48]{0,2,1:T(8,128)(2,1)S(1)} collective-permute-done((bf16[768,8,48]{0,2,1:T(8,128)(2,1)S(1)}, bf16[768,8,48]{0,2,1:T(8,128)(2,1)S(1)}, u32[]{:S(2)}, u32[]{:S(2)}) %collective-permute-start.8) | collective-permute-done | bytes 589856 | tf_op jit(solution)/shard_map/while/body/eval_jaxpr/ppermute | solution.py:28
  346.9 3.4 collective-permute-done.1
  358.2 3.4 collective-permute-done.3
  367.1 3.5 collective-permute-done.5
  376.1 3.4 collective-permute-done.7
  382.7 7.1 %collective-permute-done.8 = bf16[768,8,48]{0,2,1:T(8,128)(2,1)S(1)} collective-permute-done((bf16[768,8,48]{0,2,1:T(8,128)(2,1)S(1)}, bf16[768,8,48]{0,2,1:T(8,128)(2,1)S(1)}, u32[]{:S(2)}, u32[]{:S(2)}) %collective-permute-start.8) | collective-permute-done | bytes 589856 | tf_op jit(solution)/shard_map/while/body/eval_jaxpr/ppermute | solution.py:28
  390.1 137.9 %psum.7 = f32[48,48]{0,1:T(8,128)S(1)} all-reduce(f32[48,48]{0,1:T(8,128)S(1)} %convolution_bitcast_fusion), channel_id=1, replica_groups=mesh['section'=8,'span'=32] {'span'}, use_global_device_ids=true, to_apply=%region_2.3 | all-reduce | flops 2304 | bytes 18432 | tf_op jit(solution)/shard_map/psum | solution.py:74
  528.0 4.4 cholesky.17
  533.8 3.7 custom-call.7
  (286 shorter events, 210.0 us)
Async XLA Ops:
  2.2 10.4 %collective-permute-start = (bf16[768,1,48]{0,2,1:T(8,128)(2,1)S(1)}, bf16[768,1,48]{0,2,1:T(8,128)(2,1)S(1)}, u32[]{:S(2)}, u32[]{:S(2)}) collective-permute-start(bf16[768,1,48]{0,2,1:T(8,128)(2,1)S(1)} %get-tuple-element.284), channel_id=1, source_target_pairs={{1,0},{2,1},{3,2},{4,3},{5,4},{6,5},{7,6},{8,7},{9,8},{10,9},{11,1... | collective-permute-start | bytes 221192 | tf_op jit(solution)/shard_map/while/body/eval_jaxpr/ppermute | solution.py:20
  10.6 7.7 %collective-permute-start.1 = (bf16[768,1,48]{0,2,1:T(8,128)(2,1)S(1)}, bf16[768,1,48]{0,2,1:T(8,128)(2,1)S(1)}, u32[]{:S(2)}, u32[]{:S(2)}) collective-permute-start(bf16[768,1,48]{0,2,1:T(8,128)(2,1)S(1)} %get-tuple-element.285), channel_id=1, source_target_pairs={{0,1},{1,2},{2,3},{3,4},{4,5},{5,6},{6,7},{7,8},{8,9},{9,10},{10,1... | collective-permute-start | bytes 221192 | tf_op jit(solution)/shard_map/while/body/eval_jaxpr/ppermute | solution.py:17
  21.4 7.8 %collective-permute-start.3 = (bf16[768,1,48]{0,2,1:T(8,128)(2,1)S(1)}, bf16[768,1,48]{0,2,1:T(8,128)(2,1)S(1)}, u32[]{:S(2)}, u32[]{:S(2)}) collective-permute-start(bf16[768,1,48]{0,2,1:T(8,128)(2,1)S(1)} %get-tuple-element.288), channel_id=1, source_target_pairs={{0,1},{1,2},{2,3},{3,4},{4,5},{5,6},{6,7},{7,8},{8,9},{9,10},{10,1... | collective-permute-start | bytes 221192 | tf_op jit(solution)/shard_map/while/body/eval_jaxpr/ppermute | solution.py:17
  30.3 7.8 %collective-permute-start.5 = (bf16[768,1,48]{0,2,1:T(8,128)(2,1)S(1)}, bf16[768,1,48]{0,2,1:T(8,128)(2,1)S(1)}, u32[]{:S(2)}, u32[]{:S(2)}) collective-permute-start(bf16[768,1,48]{0,2,1:T(8,128)(2,1)S(1)} %get-tuple-element.291), channel_id=1, source_target_pairs={{0,1},{1,2},{2,3},{3,4},{4,5},{5,6},{6,7},{7,8},{8,9},{9,10},{10,1... | collective-permute-start | bytes 221192 | tf_op jit(solution)/shard_map/while/body/eval_jaxpr/ppermute | solution.py:17
  39.1 7.8 %collective-permute-start.7 = (bf16[768,1,48]{0,2,1:T(8,128)(2,1)S(1)}, bf16[768,1,48]{0,2,1:T(8,128)(2,1)S(1)}, u32[]{:S(2)}, u32[]{:S(2)}) collective-permute-start(bf16[768,1,48]{0,2,1:T(8,128)(2,1)S(1)} %get-tuple-element.294), channel_id=1, source_target_pairs={{0,1},{1,2},{2,3},{3,4},{4,5},{5,6},{6,7},{7,8},{8,9},{9,10},{10,1... | collective-permute-start | bytes 221192 | tf_op jit(solution)/shard_map/while/body/eval_jaxpr/ppermute | solution.py:17
  47.9 9.3 %collective-permute-start.8 = (bf16[768,8,48]{0,2,1:T(8,128)(2,1)S(1)}, bf16[768,8,48]{0,2,1:T(8,128)(2,1)S(1)}, u32[]{:S(2)}, u32[]{:S(2)}) collective-permute-start(bf16[768,8,48]{0,2,1:T(8,128)(2,1)S(1)} %bitcast.97), channel_id=1, source_target_pairs={{32,0},{64,32},{96,64},{128,96},{160,128},{192,160},{224,192},{33,... | collective-permute-start | bytes 1769480 | tf_op jit(solution)/shard_map/while/body/eval_jaxpr/ppermute | solution.py:28
  57.5 7.8 %collective-permute-start.1 = (bf16[768,1,48]{0,2,1:T(8,128)(2,1)S(1)}, bf16[768,1,48]{0,2,1:T(8,128)(2,1)S(1)}, u32[]{:S(2)}, u32[]{:S(2)}) collective-permute-start(bf16[768,1,48]{0,2,1:T(8,128)(2,1)S(1)} %get-tuple-element.285), channel_id=1, source_target_pairs={{0,1},{1,2},{2,3},{3,4},{4,5},{5,6},{6,7},{7,8},{8,9},{9,10},{10,1... | collective-permute-start | bytes 221192 | tf_op jit(solution)/shard_map/while/body/eval_jaxpr/ppermute | solution.py:17
  68.3 4.9 collective-permute-start.2
  68.4 8.2 %collective-permute-start.3 = (bf16[768,1,48]{0,2,1:T(8,128)(2,1)S(1)}, bf16[768,1,48]{0,2,1:T(8,128)(2,1)S(1)}, u32[]{:S(2)}, u32[]{:S(2)}) collective-permute-start(bf16[768,1,48]{0,2,1:T(8,128)(2,1)S(1)} %get-tuple-element.288), channel_id=1, source_target_pairs={{0,1},{1,2},{2,3},{3,4},{4,5},{5,6},{6,7},{7,8},{8,9},{9,10},{10,1... | collective-permute-start | bytes 221192 | tf_op jit(solution)/shard_map/while/body/eval_jaxpr/ppermute | solution.py:17
  77.9 7.7 %collective-permute-start.5 = (bf16[768,1,48]{0,2,1:T(8,128)(2,1)S(1)}, bf16[768,1,48]{0,2,1:T(8,128)(2,1)S(1)}, u32[]{:S(2)}, u32[]{:S(2)}) collective-permute-start(bf16[768,1,48]{0,2,1:T(8,128)(2,1)S(1)} %get-tuple-element.291), channel_id=1, source_target_pairs={{0,1},{1,2},{2,3},{3,4},{4,5},{5,6},{6,7},{7,8},{8,9},{9,10},{10,1... | collective-permute-start | bytes 221192 | tf_op jit(solution)/shard_map/while/body/eval_jaxpr/ppermute | solution.py:17
  86.7 7.8 %collective-permute-start.7 = (bf16[768,1,48]{0,2,1:T(8,128)(2,1)S(1)}, bf16[768,1,48]{0,2,1:T(8,128)(2,1)S(1)}, u32[]{:S(2)}, u32[]{:S(2)}) collective-permute-start(bf16[768,1,48]{0,2,1:T(8,128)(2,1)S(1)} %get-tuple-element.294), channel_id=1, source_target_pairs={{0,1},{1,2},{2,3},{3,4},{4,5},{5,6},{6,7},{7,8},{8,9},{9,10},{10,1... | collective-permute-start | bytes 221192 | tf_op jit(solution)/shard_map/while/body/eval_jaxpr/ppermute | solution.py:17
  95.4 9.3 %collective-permute-start.8 = (bf16[768,8,48]{0,2,1:T(8,128)(2,1)S(1)}, bf16[768,8,48]{0,2,1:T(8,128)(2,1)S(1)}, u32[]{:S(2)}, u32[]{:S(2)}) collective-permute-start(bf16[768,8,48]{0,2,1:T(8,128)(2,1)S(1)} %bitcast.97), channel_id=1, source_target_pairs={{32,0},{64,32},{96,64},{128,96},{160,128},{192,160},{224,192},{33,... | collective-permute-start | bytes 1769480 | tf_op jit(solution)/shard_map/while/body/eval_jaxpr/ppermute | solution.py:28
  105.0 7.8 %collective-permute-start.1 = (bf16[768,1,48]{0,2,1:T(8,128)(2,1)S(1)}, bf16[768,1,48]{0,2,1:T(8,128)(2,1)S(1)}, u32[]{:S(2)}, u32[]{:S(2)}) collective-permute-start(bf16[768,1,48]{0,2,1:T(8,128)(2,1)S(1)} %get-tuple-element.285), channel_id=1, source_target_pairs={{0,1},{1,2},{2,3},{3,4},{4,5},{5,6},{6,7},{7,8},{8,9},{9,10},{10,1... | collective-permute-start | bytes 221192 | tf_op jit(solution)/shard_map/while/body/eval_jaxpr/ppermute | solution.py:17
  115.8 4.9 collective-permute-start.2
  115.9 8.2 %collective-permute-start.3 = (bf16[768,1,48]{0,2,1:T(8,128)(2,1)S(1)}, bf16[768,1,48]{0,2,1:T(8,128)(2,1)S(1)}, u32[]{:S(2)}, u32[]{:S(2)}) collective-permute-start(bf16[768,1,48]{0,2,1:T(8,128)(2,1)S(1)} %get-tuple-element.288), channel_id=1, source_target_pairs={{0,1},{1,2},{2,3},{3,4},{4,5},{5,6},{6,7},{7,8},{8,9},{9,10},{10,1... | collective-permute-start | bytes 221192 | tf_op jit(solution)/shard_map/while/body/eval_jaxpr/ppermute | solution.py:17
  125.4 7.7 %collective-permute-start.5 = (bf16[768,1,48]{0,2,1:T(8,128)(2,1)S(1)}, bf16[768,1,48]{0,2,1:T(8,128)(2,1)S(1)}, u32[]{:S(2)}, u32[]{:S(2)}) collective-permute-start(bf16[768,1,48]{0,2,1:T(8,128)(2,1)S(1)} %get-tuple-element.291), channel_id=1, source_target_pairs={{0,1},{1,2},{2,3},{3,4},{4,5},{5,6},{6,7},{7,8},{8,9},{9,10},{10,1... | collective-permute-start | bytes 221192 | tf_op jit(solution)/shard_map/while/body/eval_jaxpr/ppermute | solution.py:17
  134.2 7.8 %collective-permute-start.7 = (bf16[768,1,48]{0,2,1:T(8,128)(2,1)S(1)}, bf16[768,1,48]{0,2,1:T(8,128)(2,1)S(1)}, u32[]{:S(2)}, u32[]{:S(2)}) collective-permute-start(bf16[768,1,48]{0,2,1:T(8,128)(2,1)S(1)} %get-tuple-element.294), channel_id=1, source_target_pairs={{0,1},{1,2},{2,3},{3,4},{4,5},{5,6},{6,7},{7,8},{8,9},{9,10},{10,1... | collective-permute-start | bytes 221192 | tf_op jit(solution)/shard_map/while/body/eval_jaxpr/ppermute | solution.py:17
  142.9 9.3 %collective-permute-start.8 = (bf16[768,8,48]{0,2,1:T(8,128)(2,1)S(1)}, bf16[768,8,48]{0,2,1:T(8,128)(2,1)S(1)}, u32[]{:S(2)}, u32[]{:S(2)}) collective-permute-start(bf16[768,8,48]{0,2,1:T(8,128)(2,1)S(1)} %bitcast.97), channel_id=1, source_target_pairs={{32,0},{64,32},{96,64},{128,96},{160,128},{192,160},{224,192},{33,... | collective-permute-start | bytes 1769480 | tf_op jit(solution)/shard_map/while/body/eval_jaxpr/ppermute | solution.py:28
  152.5 7.8 %collective-permute-start.1 = (bf16[768,1,48]{0,2,1:T(8,128)(2,1)S(1)}, bf16[768,1,48]{0,2,1:T(8,128)(2,1)S(1)}, u32[]{:S(2)}, u32[]{:S(2)}) collective-permute-start(bf16[768,1,48]{0,2,1:T(8,128)(2,1)S(1)} %get-tuple-element.285), channel_id=1, source_target_pairs={{0,1},{1,2},{2,3},{3,4},{4,5},{5,6},{6,7},{7,8},{8,9},{9,10},{10,1... | collective-permute-start | bytes 221192 | tf_op jit(solution)/shard_map/while/body/eval_jaxpr/ppermute | solution.py:17
  163.3 4.9 collective-permute-start.2
  163.4 8.2 %collective-permute-start.3 = (bf16[768,1,48]{0,2,1:T(8,128)(2,1)S(1)}, bf16[768,1,48]{0,2,1:T(8,128)(2,1)S(1)}, u32[]{:S(2)}, u32[]{:S(2)}) collective-permute-start(bf16[768,1,48]{0,2,1:T(8,128)(2,1)S(1)} %get-tuple-element.288), channel_id=1, source_target_pairs={{0,1},{1,2},{2,3},{3,4},{4,5},{5,6},{6,7},{7,8},{8,9},{9,10},{10,1... | collective-permute-start | bytes 221192 | tf_op jit(solution)/shard_map/while/body/eval_jaxpr/ppermute | solution.py:17
  172.9 7.7 %collective-permute-start.5 = (bf16[768,1,48]{0,2,1:T(8,128)(2,1)S(1)}, bf16[768,1,48]{0,2,1:T(8,128)(2,1)S(1)}, u32[]{:S(2)}, u32[]{:S(2)}) collective-permute-start(bf16[768,1,48]{0,2,1:T(8,128)(2,1)S(1)} %get-tuple-element.291), channel_id=1, source_target_pairs={{0,1},{1,2},{2,3},{3,4},{4,5},{5,6},{6,7},{7,8},{8,9},{9,10},{10,1... | collective-permute-start | bytes 221192 | tf_op jit(solution)/shard_map/while/body/eval_jaxpr/ppermute | solution.py:17
  181.7 7.8 %collective-permute-start.7 = (bf16[768,1,48]{0,2,1:T(8,128)(2,1)S(1)}, bf16[768,1,48]{0,2,1:T(8,128)(2,1)S(1)}, u32[]{:S(2)}, u32[]{:S(2)}) collective-permute-start(bf16[768,1,48]{0,2,1:T(8,128)(2,1)S(1)} %get-tuple-element.294), channel_id=1, source_target_pairs={{0,1},{1,2},{2,3},{3,4},{4,5},{5,6},{6,7},{7,8},{8,9},{9,10},{10,1... | collective-permute-start | bytes 221192 | tf_op jit(solution)/shard_map/while/body/eval_jaxpr/ppermute | solution.py:17
  190.5 9.3 %collective-permute-start.8 = (bf16[768,8,48]{0,2,1:T(8,128)(2,1)S(1)}, bf16[768,8,48]{0,2,1:T(8,128)(2,1)S(1)}, u32[]{:S(2)}, u32[]{:S(2)}) collective-permute-start(bf16[768,8,48]{0,2,1:T(8,128)(2,1)S(1)} %bitcast.97), channel_id=1, source_target_pairs={{32,0},{64,32},{96,64},{128,96},{160,128},{192,160},{224,192},{33,... | collective-permute-start | bytes 1769480 | tf_op jit(solution)/shard_map/while/body/eval_jaxpr/ppermute | solution.py:28
  200.0 7.8 %collective-permute-start.1 = (bf16[768,1,48]{0,2,1:T(8,128)(2,1)S(1)}, bf16[768,1,48]{0,2,1:T(8,128)(2,1)S(1)}, u32[]{:S(2)}, u32[]{:S(2)}) collective-permute-start(bf16[768,1,48]{0,2,1:T(8,128)(2,1)S(1)} %get-tuple-element.285), channel_id=1, source_target_pairs={{0,1},{1,2},{2,3},{3,4},{4,5},{5,6},{6,7},{7,8},{8,9},{9,10},{10,1... | collective-permute-start | bytes 221192 | tf_op jit(solution)/shard_map/while/body/eval_jaxpr/ppermute | solution.py:17
  210.8 4.9 collective-permute-start.2
  210.9 8.2 %collective-permute-start.3 = (bf16[768,1,48]{0,2,1:T(8,128)(2,1)S(1)}, bf16[768,1,48]{0,2,1:T(8,128)(2,1)S(1)}, u32[]{:S(2)}, u32[]{:S(2)}) collective-permute-start(bf16[768,1,48]{0,2,1:T(8,128)(2,1)S(1)} %get-tuple-element.288), channel_id=1, source_target_pairs={{0,1},{1,2},{2,3},{3,4},{4,5},{5,6},{6,7},{7,8},{8,9},{9,10},{10,1... | collective-permute-start | bytes 221192 | tf_op jit(solution)/shard_map/while/body/eval_jaxpr/ppermute | solution.py:17
  220.4 7.7 %collective-permute-start.5 = (bf16[768,1,48]{0,2,1:T(8,128)(2,1)S(1)}, bf16[768,1,48]{0,2,1:T(8,128)(2,1)S(1)}, u32[]{:S(2)}, u32[]{:S(2)}) collective-permute-start(bf16[768,1,48]{0,2,1:T(8,128)(2,1)S(1)} %get-tuple-element.291), channel_id=1, source_target_pairs={{0,1},{1,2},{2,3},{3,4},{4,5},{5,6},{6,7},{7,8},{8,9},{9,10},{10,1... | collective-permute-start | bytes 221192 | tf_op jit(solution)/shard_map/while/body/eval_jaxpr/ppermute | solution.py:17
  229.2 7.8 %collective-permute-start.7 = (bf16[768,1,48]{0,2,1:T(8,128)(2,1)S(1)}, bf16[768,1,48]{0,2,1:T(8,128)(2,1)S(1)}, u32[]{:S(2)}, u32[]{:S(2)}) collective-permute-start(bf16[768,1,48]{0,2,1:T(8,128)(2,1)S(1)} %get-tuple-element.294), channel_id=1, source_target_pairs={{0,1},{1,2},{2,3},{3,4},{4,5},{5,6},{6,7},{7,8},{8,9},{9,10},{10,1... | collective-permute-start | bytes 221192 | tf_op jit(solution)/shard_map/while/body/eval_jaxpr/ppermute | solution.py:17
  238.0 9.3 %collective-permute-start.8 = (bf16[768,8,48]{0,2,1:T(8,128)(2,1)S(1)}, bf16[768,8,48]{0,2,1:T(8,128)(2,1)S(1)}, u32[]{:S(2)}, u32[]{:S(2)}) collective-permute-start(bf16[768,8,48]{0,2,1:T(8,128)(2,1)S(1)} %bitcast.97), channel_id=1, source_target_pairs={{32,0},{64,32},{96,64},{128,96},{160,128},{192,160},{224,192},{33,... | collective-permute-start | bytes 1769480 | tf_op jit(solution)/shard_map/while/body/eval_jaxpr/ppermute | solution.py:28
  247.5 7.8 %collective-permute-start.1 = (bf16[768,1,48]{0,2,1:T(8,128)(2,1)S(1)}, bf16[768,1,48]{0,2,1:T(8,128)(2,1)S(1)}, u32[]{:S(2)}, u32[]{:S(2)}) collective-permute-start(bf16[768,1,48]{0,2,1:T(8,128)(2,1)S(1)} %get-tuple-element.285), channel_id=1, source_target_pairs={{0,1},{1,2},{2,3},{3,4},{4,5},{5,6},{6,7},{7,8},{8,9},{9,10},{10,1... | collective-permute-start | bytes 221192 | tf_op jit(solution)/shard_map/while/body/eval_jaxpr/ppermute | solution.py:17
  258.3 4.9 collective-permute-start.2
  258.4 8.2 %collective-permute-start.3 = (bf16[768,1,48]{0,2,1:T(8,128)(2,1)S(1)}, bf16[768,1,48]{0,2,1:T(8,128)(2,1)S(1)}, u32[]{:S(2)}, u32[]{:S(2)}) collective-permute-start(bf16[768,1,48]{0,2,1:T(8,128)(2,1)S(1)} %get-tuple-element.288), channel_id=1, source_target_pairs={{0,1},{1,2},{2,3},{3,4},{4,5},{5,6},{6,7},{7,8},{8,9},{9,10},{10,1... | collective-permute-start | bytes 221192 | tf_op jit(solution)/shard_map/while/body/eval_jaxpr/ppermute | solution.py:17
  267.9 7.7 %collective-permute-start.5 = (bf16[768,1,48]{0,2,1:T(8,128)(2,1)S(1)}, bf16[768,1,48]{0,2,1:T(8,128)(2,1)S(1)}, u32[]{:S(2)}, u32[]{:S(2)}) collective-permute-start(bf16[768,1,48]{0,2,1:T(8,128)(2,1)S(1)} %get-tuple-element.291), channel_id=1, source_target_pairs={{0,1},{1,2},{2,3},{3,4},{4,5},{5,6},{6,7},{7,8},{8,9},{9,10},{10,1... | collective-permute-start | bytes 221192 | tf_op jit(solution)/shard_map/while/body/eval_jaxpr/ppermute | solution.py:17
  276.7 7.8 %collective-permute-start.7 = (bf16[768,1,48]{0,2,1:T(8,128)(2,1)S(1)}, bf16[768,1,48]{0,2,1:T(8,128)(2,1)S(1)}, u32[]{:S(2)}, u32[]{:S(2)}) collective-permute-start(bf16[768,1,48]{0,2,1:T(8,128)(2,1)S(1)} %get-tuple-element.294), channel_id=1, source_target_pairs={{0,1},{1,2},{2,3},{3,4},{4,5},{5,6},{6,7},{7,8},{8,9},{9,10},{10,1... | collective-permute-start | bytes 221192 | tf_op jit(solution)/shard_map/while/body/eval_jaxpr/ppermute | solution.py:17
  285.5 9.3 %collective-permute-start.8 = (bf16[768,8,48]{0,2,1:T(8,128)(2,1)S(1)}, bf16[768,8,48]{0,2,1:T(8,128)(2,1)S(1)}, u32[]{:S(2)}, u32[]{:S(2)}) collective-permute-start(bf16[768,8,48]{0,2,1:T(8,128)(2,1)S(1)} %bitcast.97), channel_id=1, source_target_pairs={{32,0},{64,32},{96,64},{128,96},{160,128},{192,160},{224,192},{33,... | collective-permute-start | bytes 1769480 | tf_op jit(solution)/shard_map/while/body/eval_jaxpr/ppermute | solution.py:28
  295.0 7.8 %collective-permute-start.1 = (bf16[768,1,48]{0,2,1:T(8,128)(2,1)S(1)}, bf16[768,1,48]{0,2,1:T(8,128)(2,1)S(1)}, u32[]{:S(2)}, u32[]{:S(2)}) collective-permute-start(bf16[768,1,48]{0,2,1:T(8,128)(2,1)S(1)} %get-tuple-element.285), channel_id=1, source_target_pairs={{0,1},{1,2},{2,3},{3,4},{4,5},{5,6},{6,7},{7,8},{8,9},{9,10},{10,1... | collective-permute-start | bytes 221192 | tf_op jit(solution)/shard_map/while/body/eval_jaxpr/ppermute | solution.py:17
  305.8 4.9 collective-permute-start.2
  305.9 8.2 %collective-permute-start.3 = (bf16[768,1,48]{0,2,1:T(8,128)(2,1)S(1)}, bf16[768,1,48]{0,2,1:T(8,128)(2,1)S(1)}, u32[]{:S(2)}, u32[]{:S(2)}) collective-permute-start(bf16[768,1,48]{0,2,1:T(8,128)(2,1)S(1)} %get-tuple-element.288), channel_id=1, source_target_pairs={{0,1},{1,2},{2,3},{3,4},{4,5},{5,6},{6,7},{7,8},{8,9},{9,10},{10,1... | collective-permute-start | bytes 221192 | tf_op jit(solution)/shard_map/while/body/eval_jaxpr/ppermute | solution.py:17
  315.4 7.7 %collective-permute-start.5 = (bf16[768,1,48]{0,2,1:T(8,128)(2,1)S(1)}, bf16[768,1,48]{0,2,1:T(8,128)(2,1)S(1)}, u32[]{:S(2)}, u32[]{:S(2)}) collective-permute-start(bf16[768,1,48]{0,2,1:T(8,128)(2,1)S(1)} %get-tuple-element.291), channel_id=1, source_target_pairs={{0,1},{1,2},{2,3},{3,4},{4,5},{5,6},{6,7},{7,8},{8,9},{9,10},{10,1... | collective-permute-start | bytes 221192 | tf_op jit(solution)/shard_map/while/body/eval_jaxpr/ppermute | solution.py:17
  324.2 7.8 %collective-permute-start.7 = (bf16[768,1,48]{0,2,1:T(8,128)(2,1)S(1)}, bf16[768,1,48]{0,2,1:T(8,128)(2,1)S(1)}, u32[]{:S(2)}, u32[]{:S(2)}) collective-permute-start(bf16[768,1,48]{0,2,1:T(8,128)(2,1)S(1)} %get-tuple-element.294), channel_id=1, source_target_pairs={{0,1},{1,2},{2,3},{3,4},{4,5},{5,6},{6,7},{7,8},{8,9},{9,10},{10,1... | collective-permute-start | bytes 221192 | tf_op jit(solution)/shard_map/while/body/eval_jaxpr/ppermute | solution.py:17
  333.0 9.3 %collective-permute-start.8 = (bf16[768,8,48]{0,2,1:T(8,128)(2,1)S(1)}, bf16[768,8,48]{0,2,1:T(8,128)(2,1)S(1)}, u32[]{:S(2)}, u32[]{:S(2)}) collective-permute-start(bf16[768,8,48]{0,2,1:T(8,128)(2,1)S(1)} %bitcast.97), channel_id=1, source_target_pairs={{32,0},{64,32},{96,64},{128,96},{160,128},{192,160},{224,192},{33,... | collective-permute-start | bytes 1769480 | tf_op jit(solution)/shard_map/while/body/eval_jaxpr/ppermute | solution.py:28
  342.6 7.8 %collective-permute-start.1 = (bf16[768,1,48]{0,2,1:T(8,128)(2,1)S(1)}, bf16[768,1,48]{0,2,1:T(8,128)(2,1)S(1)}, u32[]{:S(2)}, u32[]{:S(2)}) collective-permute-start(bf16[768,1,48]{0,2,1:T(8,128)(2,1)S(1)} %get-tuple-element.285), channel_id=1, source_target_pairs={{0,1},{1,2},{2,3},{3,4},{4,5},{5,6},{6,7},{7,8},{8,9},{9,10},{10,1... | collective-permute-start | bytes 221192 | tf_op jit(solution)/shard_map/while/body/eval_jaxpr/ppermute | solution.py:17
  353.3 4.9 collective-permute-start.2
  353.4 8.2 %collective-permute-start.3 = (bf16[768,1,48]{0,2,1:T(8,128)(2,1)S(1)}, bf16[768,1,48]{0,2,1:T(8,128)(2,1)S(1)}, u32[]{:S(2)}, u32[]{:S(2)}) collective-permute-start(bf16[768,1,48]{0,2,1:T(8,128)(2,1)S(1)} %get-tuple-element.288), channel_id=1, source_target_pairs={{0,1},{1,2},{2,3},{3,4},{4,5},{5,6},{6,7},{7,8},{8,9},{9,10},{10,1... | collective-permute-start | bytes 221192 | tf_op jit(solution)/shard_map/while/body/eval_jaxpr/ppermute | solution.py:17
  362.9 7.7 %collective-permute-start.5 = (bf16[768,1,48]{0,2,1:T(8,128)(2,1)S(1)}, bf16[768,1,48]{0,2,1:T(8,128)(2,1)S(1)}, u32[]{:S(2)}, u32[]{:S(2)}) collective-permute-start(bf16[768,1,48]{0,2,1:T(8,128)(2,1)S(1)} %get-tuple-element.291), channel_id=1, source_target_pairs={{0,1},{1,2},{2,3},{3,4},{4,5},{5,6},{6,7},{7,8},{8,9},{9,10},{10,1... | collective-permute-start | bytes 221192 | tf_op jit(solution)/shard_map/while/body/eval_jaxpr/ppermute | solution.py:17
  371.7 7.8 %collective-permute-start.7 = (bf16[768,1,48]{0,2,1:T(8,128)(2,1)S(1)}, bf16[768,1,48]{0,2,1:T(8,128)(2,1)S(1)}, u32[]{:S(2)}, u32[]{:S(2)}) collective-permute-start(bf16[768,1,48]{0,2,1:T(8,128)(2,1)S(1)} %get-tuple-element.294), channel_id=1, source_target_pairs={{0,1},{1,2},{2,3},{3,4},{4,5},{5,6},{6,7},{7,8},{8,9},{9,10},{10,1... | collective-permute-start | bytes 221192 | tf_op jit(solution)/shard_map/while/body/eval_jaxpr/ppermute | solution.py:17
  380.5 9.3 %collective-permute-start.8 = (bf16[768,8,48]{0,2,1:T(8,128)(2,1)S(1)}, bf16[768,8,48]{0,2,1:T(8,128)(2,1)S(1)}, u32[]{:S(2)}, u32[]{:S(2)}) collective-permute-start(bf16[768,8,48]{0,2,1:T(8,128)(2,1)S(1)} %bitcast.97), channel_id=1, source_target_pairs={{32,0},{64,32},{96,64},{128,96},{160,128},{192,160},{224,192},{33,... | collective-permute-start | bytes 1769480 | tf_op jit(solution)/shard_map/while/body/eval_jaxpr/ppermute | solution.py:28
  (33 other events, 126.4 us)
where the time goes:
time: 544 us
  waiting for transfers between devices  246 us (45%)
  blocking collectives  138 us (25%)
  starting transfers between devices  88.8 us (16%)
  matrix products  23.6 us (4%)
  other arithmetic  23 us (4%)
  local copies, waits for them, and re-layouts  22.5 us (4%)
    psum x1, blocking collectives, local(): summed = lax.psum(partial_gram, 'span')  138 us
    ppermute x32, waiting for transfers between devices, padded(): lax.ppermute(lax.slice_in_dim(block, block.shape[dim] - width, None, axis...  112 us
    ppermute x32, waiting for transfers between devices, padded(): lax.ppermute(lax.slice_in_dim(block, 0, width, axis=dim), axis, backward)  76.8 us
    ppermute x32, starting transfers between devices, padded(): lax.ppermute(lax.slice_in_dim(block, block.shape[dim] - width, None, axis...  61.1 us
    ppermute x8, waiting for transfers between devices, from_behind(): return lax.ppermute(value, axis, pairs)  57 us
    dot_general x32, matrix products, apply_station(): jnp.dot(blocks, update.reshape(blocks.shape[0], -1), preferred_element_ty...  21.4 us
    while x16, local copies, waits for them, and re-layouts  16 us
    ppermute x8, starting transfers between devices, from_behind(): return lax.ppermute(value, axis, pairs)  15.4 us
  transfers between devices with their start and end apart: 72, of which 72 were waited for; matrix products, arithmetic and copies ran while one was open for 0% of the time, Pallas kernels for 0%

commit v1 on v0

v1 whole, which is shorter than its diff:
```python
import functools

import jax
import jax.numpy as jnp
from jax import lax
from jax.experimental import pallas as pl
from jax.experimental.pallas import tpu as pltpu
from jax.sharding import PartitionSpec as P

MESH = pl.DeviceIdType.MESH
K = 48
STATIONS = 4
KC = 16
CHUNKS = K // KC
BF = jnp.bfloat16
F32 = jnp.float32


def grid_sizes(mesh):
    span = mesh.shape["span"]
    rows = 4 if span == 32 else 2
    return mesh.shape["section"], rows, span // rows


def march_kernel(sizes, lz, fn, a_hbm, c_ref, s_hbm, yt_ref, g_ref,
                 av, at, sv, st, ext, inc, wa, wb, yv, gy, gz,
                 lsem, msend, mrecv, hsend, hrecv, ysend, yrecv, zsend, zrecv):
    ng, ny, nz = sizes
    ns = ny * nz
    rows = lz * KC
    halo = STATIONS * KC
    g = lax.axis_index("section")
    s = lax.axis_index("span")
    my, mz = s // nz, lax.rem(s, nz)
    left = (g, lax.rem(s + ns - 1, ns))
    right = (g, lax.rem(s + 1, ns))
    last = g == ng - 1

    source_copy = pltpu.make_async_copy(s_hbm, sv, lsem.at[STATIONS])
    source_copy.start()
    weight_copies = [pltpu.make_async_copy(a_hbm.at[i], av.at[i], lsem.at[i]) for i in range(STATIONS)]
    for i in reversed(range(STATIONS)):
        weight_copies[i].start()

    barrier = pltpu.get_barrier_semaphore()

    def greet(device):
        pl.semaphore_signal(barrier, inc=1, device_id=device, device_id_type=MESH)

    y_peer = lambda d: (g, lax.rem(my + d, ny) * nz + mz)
    z_peer = lambda d: (g, my * nz + lax.rem(mz + d, nz))
    greet(left)
    greet(right)
    for d in range(1, ny):
        greet(y_peer(d))
    for d in range(1, nz):
        greet(z_peer(d))

    greet((lax.rem(g + ng - 1, ng), s))
    greet((lax.rem(g + 1, ng), s))

    source_copy.wait()
    wide_row = lax.broadcasted_iota(jnp.int32, (rows, lz * K), 0)
    wide_lane = lax.broadcasted_iota(jnp.int32, (rows, lz * K), 1)
    for c in range(CHUNKS):
        pick = (wide_lane == (wide_row // KC) * K + c * KC + lax.rem(wide_row, KC)).astype(F32).astype(BF)
        st[c] = lax.dot_general(pick, sv[...], (((1,), (1,)), ((), ())), preferred_element_type=F32).astype(BF)

    pl.semaphore_wait(barrier, ny + nz + 2)

    def main_copy(c):
        return pltpu.make_async_remote_copy(
            src_ref=yv.at[c], dst_ref=inc.at[c], send_sem=msend.at[c], recv_sem=mrecv.at[c],
            device_id=(lax.rem(g + ng - 1, ng), s), device_id_type=MESH)

    def halo_copy(c, side):
        start, target, device = ((halo, halo + rows, left), (rows, 0, right))[side]
        return pltpu.make_async_remote_copy(
            src_ref=ext.at[c, pl.ds(start, halo)], dst_ref=ext.at[c, pl.ds(target, halo)],
            send_sem=hsend.at[c, side], recv_sem=hrecv.at[c, side],
            device_id=device, device_id_type=MESH)

    @pl.when(last)
    def _():
        for c in range(CHUNKS):
            ext[c, pl.ds(halo, rows), :] = st[c]
            halo_copy(c, 0).start()
            halo_copy(c, 1).start()

    for i in reversed(range(STATIONS)):
        weight_copies[i].wait()
        at[i] = av[i].T

    def prepare(c):
        @pl.when(jnp.logical_not(last))
        def _():
            main_copy(c).wait_recv()
            ext[c, pl.ds(halo, rows), :] = (inc[c].astype(F32) + st[c].astype(F32)).astype(BF)
            halo_copy(c, 0).start()
            halo_copy(c, 1).start()

    def station(index, value, count, store):
        w = value.astype(F32)
        center = w[KC:-KC]
        spread = w[2 * KC:] + w[:-2 * KC] - 2.0 * center
        update = (center + c_ref[index:index + 1, :] * spread).astype(BF)
        store(jnp.dot(update, at[index], preferred_element_type=F32).astype(BF))

    def put(ref, *where):
        def store(v):
            ref[where] = v
        return store

    def compute(c):
        n = rows + 2 * halo
        step = 2 * KC
        halo_copy(c, 0).wait_recv()
        halo_copy(c, 1).wait_recv()
        station(3, ext[c], n - step, put(wa, pl.ds(0, n - step), slice(None)))
        station(2, wa[pl.ds(0, n - step), :], n - 2 * step, put(wb, pl.ds(0, n - 2 * step), slice(None)))
        station(1, wb[pl.ds(0, n - 2 * step), :], n - 3 * step, put(wa, pl.ds(0, n - 3 * step), slice(None)))
        station(0, wa[pl.ds(0, n - 3 * step), :], n - 4 * step, put(yv, c))

        @pl.when(g > 0)
        def _():
            main_copy(c).start()

    prepare(0)

    def chunk_step(c, carry):
        @pl.when(c < CHUNKS - 1)
        def _():
            prepare(c + 1)

        compute(c)
        return carry

    lax.fori_loop(0, CHUNKS, chunk_step, 0)

    total = CHUNKS * rows
    flat = yv[...].reshape(total, fn)
    gram = lax.dot_general(flat, flat, (((1,), (1,)), ((), ())), preferred_element_type=F32)
    z_of_row = lax.rem(lax.broadcasted_iota(jnp.int32, (total, total), 0), rows) // KC
    z_of_lane = lax.rem(lax.broadcasted_iota(jnp.int32, (total, total), 1), rows) // KC
    gram = jnp.where(z_of_row == z_of_lane, gram, 0.0)
    gram = gram.reshape(CHUNKS, lz, KC, total).sum(1).reshape(K, total)
    lane = lax.broadcasted_iota(jnp.int32, (K, rows), 1)
    packed = jnp.zeros((K, rows), F32)
    for c in range(CHUNKS):
        tile = gram[:, c * rows:(c + 1) * rows]
        shift = rows // 2
        while shift >= KC:
            tile = tile + pltpu.roll(tile, shift, 1)
            shift //= 2
        packed = jnp.where(lane // KC == c, tile, packed)

    gy[my] = packed

    def y_copy(d):
        return pltpu.make_async_remote_copy(
            src_ref=gy.at[my], dst_ref=gy.at[my], send_sem=ysend.at[d - 1], recv_sem=yrecv.at[d - 1],
            device_id=y_peer(d), device_id_type=MESH)

    def z_copy(d):
        return pltpu.make_async_remote_copy(
            src_ref=gz.at[mz], dst_ref=gz.at[mz], send_sem=zsend.at[d - 1], recv_sem=zrecv.at[d - 1],
            device_id=z_peer(d), device_id_type=MESH)

    for d in range(1, ny):
        y_copy(d).start()
    yt_ref[...] = flat.T
    for d in range(1, ny):
        y_copy(d).wait_recv()
    acc = gy[0]
    for i in range(1, ny):
        acc = acc + gy[i]
    gz[mz] = acc
    for d in range(1, nz):
        z_copy(d).start()
    for d in range(1, nz):
        z_copy(d).wait_recv()
    acc = gz[0]
    for i in range(1, nz):
        acc = acc + gz[i]
    g_ref[...] = acc

    for c in range(CHUNKS):
        halo_copy(c, 0).wait_send()
        halo_copy(c, 1).wait_send()

        @pl.when(g > 0)
        def _():
            main_copy(c).wait_send()

    for d in range(1, ny):
        y_copy(d).wait_send()
    for d in range(1, nz):
        z_copy(d).wait_send()


def basis_kernel(lz, count, yt_ref, g_ref, o_ref, u_ref):
    rows = lz * KC
    lane = lax.broadcasted_iota(jnp.int32, (K, 128), 1)
    row = lax.broadcasted_iota(jnp.int32, (K, 128), 0)
    scaled = g_ref[...] * (1.0 / count)
    w = jnp.where(lane < K, scaled, jnp.where(lane == row + 64, 1.0, 0.0))
    for j in range(K):
        pivot = w[j:j + 1, :]
        inv = lax.rsqrt(w[j:j + 1, j:j + 1])
        unit = pivot * inv
        column = w[:, j:j + 1] * inv
        w = jnp.where(row == j, unit, w - jnp.where(row > j, column, 0.0) * unit)
    u_ref[...] = jnp.where(lane >= row, w, 0.0)[:, :K]
    tile_row = lax.broadcasted_iota(jnp.int32, (K, lz * K), 0)
    tile_lane = lax.broadcasted_iota(jnp.int32, (K, lz * K), 1)
    spread = (tile_row == lax.rem(tile_lane, K)).astype(F32).astype(BF)
    high = w.astype(BF)
    low = (w - high.astype(F32)).astype(BF)
    block_row = lax.broadcasted_iota(jnp.int32, (rows, lz * K), 0)
    block_lane = lax.broadcasted_iota(jnp.int32, (rows, lz * K), 1)
    same = block_row // KC == block_lane // K
    out = None
    for part in (high, low):
        tiled = lax.dot_general(part, spread, (((0,), (0,)), ((), ())), preferred_element_type=F32)
        blocks = []
        for c in range(CHUNKS):
            one = tiled[64 + c * KC:64 + (c + 1) * KC]
            blocks.append(jnp.where(same, jnp.concatenate([one] * lz, axis=0), 0.0))
        block = jnp.concatenate(blocks, axis=0).astype(BF)
        term = jnp.dot(yt_ref[...], block, preferred_element_type=F32)
        out = term if out is None else out + term
    o_ref[...] = out.astype(BF)


def local(sizes, count, inverse_blocks, coupling, sources):
    ng, ny, nz = sizes
    fn = inverse_blocks.shape[1]
    lz = sources.shape[2] // K
    rows = lz * KC
    halo = STATIONS * KC
    n = rows + 2 * halo
    hbm = pl.BlockSpec(memory_space=pl.ANY)
    vmem = pl.BlockSpec(memory_space=pltpu.VMEM)
    dma = pltpu.SemaphoreType.DMA
    yt, gram = pl.pallas_call(
        functools.partial(march_kernel, sizes, lz, fn),
        name="march",
        out_shape=(jax.ShapeDtypeStruct((fn, CHUNKS * rows), BF), jax.ShapeDtypeStruct((K, 128), F32)),
        in_specs=[hbm, vmem, hbm],
        out_specs=(vmem, vmem),
        scratch_shapes=[
            pltpu.VMEM((STATIONS, fn, fn), BF),
            pltpu.VMEM((STATIONS, fn, fn), BF),
            pltpu.VMEM((fn, lz * K), BF),
            pltpu.VMEM((CHUNKS, rows, fn), BF),
            pltpu.VMEM((CHUNKS, n, fn), BF),
            pltpu.VMEM((CHUNKS, rows, fn), BF),
            pltpu.VMEM((n, fn), BF),
            pltpu.VMEM((n, fn), BF),
            pltpu.VMEM((CHUNKS, rows, fn), BF),
            pltpu.VMEM((ny, K, 128), F32),
            pltpu.VMEM((nz, K, 128), F32),
            dma((STATIONS + 1,)),
            dma((CHUNKS,)),
            dma((CHUNKS,)),
            dma((CHUNKS, 2)),
            dma((CHUNKS, 2)),
            dma((ny - 1,)),
            dma((ny - 1,)),
            dma((nz - 1,)),
            dma((nz - 1,)),
        ],
        compiler_params=pltpu.CompilerParams(collective_id=0, has_side_effects=True, vmem_limit_bytes=48 << 20),
    )(inverse_blocks, coupling, sources[0])
    basis, upper = pl.pallas_call(
        functools.partial(basis_kernel, lz, count),
        name="basis",
        out_shape=(jax.ShapeDtypeStruct((fn, lz * K), BF), jax.ShapeDtypeStruct((K, K), F32)),
        in_specs=[vmem, vmem],
        out_specs=(vmem, vmem),
        compiler_params=pltpu.CompilerParams(vmem_limit_bytes=48 << 20),
    )(yt, gram)
    return basis[None], upper[None]


def solution(mesh):
    placed = (P("section", None, None), P("section", None), P("section", None, "span"))
    sizes = grid_sizes(mesh)

    def whole(inverse_blocks, coupling, sources):
        count = float(sources.shape[1] * sources.shape[2] // K)
        return jax.shard_map(
            functools.partial(local, sizes, count),
            mesh=mesh,
            in_specs=placed,
            out_specs=(P("section", None, "span"), P("section", None, None)),
            check_vma=False,
        )(inverse_blocks, coupling, sources)

    return whole
```

time: 544 us -> 107 us (0.20)
  the two profiles are of different devices: /device:TPU:2 before, /device:TPU:32 now
where the time goes in v1:
time: 107 us; the launch traced here: 106 us
  Pallas kernels  102 us (95%)
  local copies, waits for them, and re-layouts  4.1 us (4%)
    pallas_call x1, Pallas kernels, local(): pl.pallas_call(functools.partial(march_kernel, sizes, lz, fn), name='marc...  95.8 us
    pallas_call x1, Pallas kernels, local(): pl.pallas_call(functools.partial(basis_kernel, lz, count), name='basis',...  5.9 us
    unnamed x6, local copies, waits for them, and re-layouts  4.1 us

profile of v1, /device:TPU:32, one launch (start us, length us, event | category | flops | bytes accessed | tf_op | source)
XLA Modules:
  0.0 106.5 jit_solution(4194044169143139521)
XLA Ops:
  0.6 0.0 copy-start
  0.6 2.3 %copy-done = bf16[4,768,768]{2,1,0:T(8,128)(2,1)S(1)} copy-done((bf16[4,768,768]{2,1,0:T(8,128)(2,1)S(1)}, bf16[4,768,768]{2,1,0:T(8,128)(2,1)}, u32[]{:S(2)}) %copy-start) | copy-done | bytes 4718616
  3.0 0.0 copy-start.1
  3.0 1.1 copy-done.1
  4.0 0.0 copy-start.2
  4.0 0.7 copy-done.2
  4.7 95.8 %march.1 = (bf16[768,384]{1,0:T(8,128)(2,1)S(1)}, f32[48,128]{1,0:T(8,128)S(1)}) custom-call(bf16[4,768,768]{2,1,0:T(8,128)(2,1)S(1)} %copy-done, f32[4,768]{1,0:T(4,128)S(1)} %copy-done.2, bf16[768,384]{1,0:T(8,128)(2,1)S(1)} %bitcast.3), custom_call_target="tpu_custom_call" | custom-call | tf_op jit(solution)/shard_map/march/pallas_call | solution.py:245
  100.6 5.9 %basis.1 = (bf16[768,384]{1,0:T(8,128)(2,1)}, f32[48,48]{1,0:T(8,128)}) custom-call(bf16[768,384]{1,0:T(8,128)(2,1)S(1)} %get-tuple-element.6.yt_ref, f32[48,128]{1,0:T(8,128)S(1)} %get-tuple-element.7.g_ref), custom_call_target="tpu_custom_call" | custom-call | tf_op jit(solution)/shard_map/basis/pallas_call | solution.py:275
Async XLA Ops:
  0.6 2.3 %copy-start = (bf16[4,768,768]{2,1,0:T(8,128)(2,1)S(1)}, bf16[4,768,768]{2,1,0:T(8,128)(2,1)}, u32[]{:S(2)}) copy-start(bf16[4,768,768]{2,1,0:T(8,128)(2,1)} %a_hbm.1) | copy-start | bytes 14155780
  3.0 1.1 copy-start.1
  4.0 0.7 copy-start.2

commit v2 on v1

v2 whole, which is shorter than its diff:
```python
import functools

import jax
import jax.numpy as jnp
from jax import lax
from jax.experimental import pallas as pl
from jax.experimental.pallas import tpu as pltpu
from jax.sharding import PartitionSpec as P

MESH = pl.DeviceIdType.MESH
K = 48
STATIONS = 4
KC = 8
CHUNKS = 3
BF = jnp.bfloat16
F32 = jnp.float32


def grid_sizes(mesh):
    span = mesh.shape["span"]
    rows = 4 if span == 32 else 2
    return mesh.shape["section"], rows, span // rows


def march_kernel(sizes, lz, fn, a_hbm, c_hbm, s_hbm, yt_ref, g_ref,
                 av, at, cv, cc, sv, tmp, sa, sb, ext, inc, wa, wb, ym, yf, gy, gz,
                 lsem, wsend, wrecv, csend, crecv, ssend, srecv, bsend, brecv,
                 msend, mrecv, hsend, hrecv, xsend, xrecv, ysend, yrecv, zsend, zrecv):
    ng, ny, nz = sizes
    ns = ny * nz
    rows = lz * KC
    half = STATIONS * KC
    g = lax.axis_index("section")
    s = lax.axis_index("span")
    core = lax.rem(g, 2)
    my, mz = s // nz, lax.rem(s, nz)
    left = (g, lax.rem(s + ns - 1, ns))
    right = (g, lax.rem(s + 1, ns))
    other = (g + 1 - 2 * core, s)
    below = (lax.rem(g + ng - 2, ng), s)
    above = (lax.rem(g + 2, ng), s)
    first_chip = g >= ng - 2
    last_chip = g < 2
    is_one = core == 1
    is_zero = core == 0

    source_copy = pltpu.make_async_copy(s_hbm, sv, lsem.at[STATIONS])
    source_copy.start()
    rate_copy = pltpu.make_async_copy(c_hbm, cv, lsem.at[STATIONS + 1])
    rate_copy.start()
    weight_copies = [pltpu.make_async_copy(a_hbm.at[i], av.at[i], lsem.at[i]) for i in range(STATIONS)]
    for i in reversed(range(STATIONS)):
        weight_copies[i].start()

    barrier = pltpu.get_barrier_semaphore()

    def greet(device):
        pl.semaphore_signal(barrier, inc=1, device_id=device, device_id_type=MESH)

    y_peer = lambda d: (g, lax.rem(my + d, ny) * nz + mz)
    z_peer = lambda d: (g, my * nz + lax.rem(mz + d, nz))
    for device in [left, right, other, below, above]:
        greet(device)
    for d in range(1, ny):
        greet(y_peer(d))
    for d in range(1, nz):
        greet(z_peer(d))

    def remote(src, dst, send, recv, device):
        return pltpu.make_async_remote_copy(
            src_ref=src, dst_ref=dst, send_sem=send, recv_sem=recv, device_id=device, device_id_type=MESH)

    weight_cross = lambda p, i: remote(at.at[p, i], at.at[p, i], wsend.at[i], wrecv.at[i], other)
    rate_cross = lambda p: remote(cc.at[p], cc.at[p], csend.at[0], crecv.at[0], other)
    middle = pl.ds(half, rows)
    source_cross_a = lambda j: remote(tmp.at[j], sa.at[j], ssend.at[j], srecv.at[j], other)
    source_cross_b = lambda j: remote(tmp.at[j], sb.at[j, middle], ssend.at[j], srecv.at[j], other)
    main_copy = lambda j: remote(ym.at[0, j], inc.at[j], msend.at[j], mrecv.at[j], below)
    cross_y = lambda j: remote(ym.at[1 - core, j], yf.at[core, j], xsend.at[j], xrecv.at[j], other)

    def halo_copy(j, side):
        target, device = ((2 * rows, left), (0, right))[side]
        return remote(ext.at[j, pl.ds(rows, rows)], ext.at[j, pl.ds(target, rows)],
                      hsend.at[j, side], hrecv.at[j, side], device)

    def source_halo(j, side):
        start, target, device = ((half, half + rows, left), (rows, 0, right))[side]
        return remote(sb.at[j, pl.ds(start, half)], sb.at[j, pl.ds(target, half)],
                      bsend.at[j, side], brecv.at[j, side], device)

    source_copy.wait()
    wide_row = lax.broadcasted_iota(jnp.int32, (rows, lz * K), 0)
    wide_lane = lax.broadcasted_iota(jnp.int32, (rows, lz * K), 1)
    base_lane = (wide_row // KC) * K + lax.rem(wide_row, KC)

    def columns(h, j):
        pick = (wide_lane == base_lane + (h * (K // 2) + j * KC)).astype(F32).astype(BF)
        return lax.dot_general(pick, sv[...], (((1,), (1,)), ((), ())), preferred_element_type=F32).astype(BF)

    for j in range(CHUNKS):
        tmp[j] = columns(1 - core, j)
        mine = columns(core, j)

        @pl.when(is_one)
        def _():
            sa[j] = mine

        @pl.when(is_zero)
        def _():
            sb[j, middle, :] = mine

    rate_copy.wait()
    cc[core] = jnp.concatenate([cv[...], jnp.zeros_like(cv)], axis=0)
    pl.semaphore_wait(barrier, ny + nz + 3)

    for j in range(CHUNKS):
        @pl.when(is_one)
        def _():
            source_cross_a(j).start()

        @pl.when(is_zero)
        def _():
            source_cross_b(j).start()

    rate_cross(core).start()

    @pl.when(first_chip)
    def _():
        for j in range(CHUNKS):
            @pl.when(is_zero)
            def _():
                source_cross_a(j).wait_recv()

            ext[j, pl.ds(rows, rows), :] = sa[j]
            halo_copy(j, 0).start()
            halo_copy(j, 1).start()

    for i in reversed(range(STATIONS)):
        weight_copies[i].wait()
        at[core, i] = av[i].T
        weight_cross(core, i).start()

    for j in range(CHUNKS):
        @pl.when(is_one)
        def _():
            source_cross_b(j).wait_recv()

        @pl.when(jnp.logical_and(is_zero, jnp.logical_not(first_chip)))
        def _():
            source_cross_a(j).wait_recv()

        source_halo(j, 0).start()
        source_halo(j, 1).start()

    rate_cross(1 - core).wait_recv()

    def prepare(j):
        @pl.when(jnp.logical_not(first_chip))
        def _():
            main_copy(j).wait_recv()
            ext[j, pl.ds(rows, rows), :] = (inc[j].astype(F32) + sa[j].astype(F32)).astype(BF)
            halo_copy(j, 0).start()
            halo_copy(j, 1).start()

    def station(j, p, i, value):
        @pl.when(jnp.logical_and(j == 0, core != p))
        def _():
            weight_cross(p, i).wait_recv()

        w = value.astype(F32)
        center = w[KC:-KC]
        spread = w[2 * KC:] + w[:-2 * KC] - 2.0 * center
        update = (center + cc[p, i:i + 1, :] * spread).astype(BF)
        return jnp.dot(update, at[p, i], preferred_element_type=F32).astype(BF)

    def compute(j):
        n = 3 * rows
        step = 2 * KC
        halo_copy(j, 0).wait_recv()
        halo_copy(j, 1).wait_recv()
        wa[pl.ds(0, n - step), :] = station(j, 1, 3, ext[j])
        wb[pl.ds(0, n - 2 * step), :] = station(j, 1, 2, wa[pl.ds(0, n - step), :])
        wa[pl.ds(0, n - 3 * step), :] = station(j, 1, 1, wb[pl.ds(0, n - 2 * step), :])
        n = 2 * rows
        upper_out = station(j, 1, 0, wa[pl.ds(0, n + step), :])
        wb[pl.ds(0, n), :] = upper_out
        ym[1, j] = wb[middle, :]

        @pl.when(is_one)
        def _():
            yf[1, j] = ym[1, j]

        @pl.when(is_zero)
        def _():
            cross_y(j).start()

        source_halo(j, 0).wait_recv()
        source_halo(j, 1).wait_recv()
        value = (upper_out.astype(F32) + sb[j].astype(F32)).astype(BF)
        wa[pl.ds(0, n - step), :] = station(j, 0, 3, value)
        wb[pl.ds(0, n - 2 * step), :] = station(j, 0, 2, wa[pl.ds(0, n - step), :])
        wa[pl.ds(0, n - 3 * step), :] = station(j, 0, 1, wb[pl.ds(0, n - 2 * step), :])
        ym[0, j] = station(j, 0, 0, wa[pl.ds(0, n - 3 * step), :])

        @pl.when(jnp.logical_not(last_chip))
        def _():
            main_copy(j).start()

        @pl.when(is_zero)
        def _():
            yf[0, j] = ym[0, j]

        @pl.when(is_one)
        def _():
            cross_y(j).start()

    prepare(0)

    def chunk_step(j, carry):
        @pl.when(j < CHUNKS - 1)
        def _():
            prepare(j + 1)

        compute(j)
        return carry

    lax.fori_loop(0, CHUNKS, chunk_step, 0)
    for j in range(CHUNKS):
        cross_y(j).wait_recv()

    total = 2 * CHUNKS * rows
    flat = yf[...].reshape(total, fn)
    gram = lax.dot_general(flat, flat, (((1,), (1,)), ((), ())), preferred_element_type=F32)
    z_of_row = lax.rem(lax.broadcasted_iota(jnp.int32, (total, total), 0), rows) // KC
    z_of_lane = lax.rem(lax.broadcasted_iota(jnp.int32, (total, total), 1), rows) // KC
    gram = jnp.where(z_of_row == z_of_lane, gram, 0.0)
    gram = gram.reshape(2 * CHUNKS, lz, KC, total).sum(1).reshape(K, total)
    lane = lax.broadcasted_iota(jnp.int32, (K, 128), 1)
    packed = jnp.zeros((K, 128), F32)
    for c in range(2 * CHUNKS):
        pair = gram[:, (c // 2) * 128:(c // 2 + 1) * 128]
        tile = jnp.where(lane // rows == c % 2, pair, 0.0)
        for shift in (64, 32, 16, 8):
            tile = tile + pltpu.roll(tile, shift, 1)
        packed = jnp.where(lane // KC == c, tile, packed)
    gy[my] = packed[:K // 2] + pltpu.roll(packed[K // 2:], 64, 1)

    y_copy = lambda d: remote(gy.at[my], gy.at[my], ysend.at[d - 1], yrecv.at[d - 1], y_peer(d))
    z_copy = lambda d: remote(gz.at[mz], gz.at[mz], zsend.at[d - 1], zrecv.at[d - 1], z_peer(d))

    for d in range(1, ny):
        y_copy(d).start()
    yt_ref[...] = flat.T
    for d in range(1, ny):
        y_copy(d).wait_recv()
    acc = gy[0]
    for i in range(1, ny):
        acc = acc + gy[i]
    gz[mz] = acc
    for d in range(1, nz):
        z_copy(d).start()
    for d in range(1, nz):
        z_copy(d).wait_recv()
    acc = gz[0]
    for i in range(1, nz):
        acc = acc + gz[i]
    g_ref[...] = acc

    rate_cross(core).wait_send()
    for i in range(STATIONS):
        weight_cross(core, i).wait_send()
    for j in range(CHUNKS):
        source_cross_a(j).wait_send()
        for side in (0, 1):
            halo_copy(j, side).wait_send()
            source_halo(j, side).wait_send()
        cross_y(j).wait_send()

        @pl.when(jnp.logical_not(last_chip))
        def _():
            main_copy(j).wait_send()

    for d in range(1, ny):
        y_copy(d).wait_send()
    for d in range(1, nz):
        z_copy(d).wait_send()


def basis_kernel(lz, count, yt_ref, g_ref, o_ref, u_ref):
    rows = lz * KC
    lane = lax.broadcasted_iota(jnp.int32, (K, 128), 1)
    row = lax.broadcasted_iota(jnp.int32, (K, 128), 0)
    gram = jnp.concatenate([g_ref[...], pltpu.roll(g_ref[...], 64, 1)], axis=0)
    scaled = gram * (1.0 / count)
    w = jnp.where(lane < K, scaled, jnp.where(lane == row + 64, 1.0, 0.0))
    for j in range(K):
        pivot = w[j:j + 1, :]
        inv = lax.rsqrt(w[j:j + 1, j:j + 1])
        unit = pivot * inv
        column = w[:, j:j + 1] * inv
        w = jnp.where(row == j, unit, w - jnp.where(row > j, column, 0.0) * unit)
    u_ref[...] = jnp.where(lane >= row, w, 0.0)[:, :K]
    tile_row = lax.broadcasted_iota(jnp.int32, (K, lz * K), 0)
    tile_lane = lax.broadcasted_iota(jnp.int32, (K, lz * K), 1)
    spread = (tile_row == lax.rem(tile_lane, K)).astype(F32).astype(BF)
    high = w.astype(BF)
    low = (w - high.astype(F32)).astype(BF)
    block_row = lax.broadcasted_iota(jnp.int32, (rows, lz * K), 0)
    block_lane = lax.broadcasted_iota(jnp.int32, (rows, lz * K), 1)
    same = block_row // KC == block_lane // K
    out = None
    for part in (high, low):
        tiled = lax.dot_general(part, spread, (((0,), (0,)), ((), ())), preferred_element_type=F32)
        blocks = []
        for c in range(2 * CHUNKS):
            one = tiled[64 + c * KC:64 + (c + 1) * KC]
            blocks.append(jnp.where(same, jnp.concatenate([one] * lz, axis=0), 0.0))
        block = jnp.concatenate(blocks, axis=0).astype(BF)
        term = jnp.dot(yt_ref[...], block, preferred_element_type=F32)
        out = term if out is None else out + term
    o_ref[...] = out.astype(BF)


def local(sizes, count, inverse_blocks, coupling, sources):
    ng, ny, nz = sizes
    fn = inverse_blocks.shape[1]
    lz = sources.shape[2] // K
    rows = lz * KC
    half = STATIONS * KC
    hbm = pl.BlockSpec(memory_space=pltpu.HBM)
    vmem = pl.BlockSpec(memory_space=pltpu.VMEM)
    dma = pltpu.SemaphoreType.DMA
    yt, gram = pl.pallas_call(
        functools.partial(march_kernel, sizes, lz, fn),
        name="march",
        out_shape=(jax.ShapeDtypeStruct((fn, lz * K), BF), jax.ShapeDtypeStruct((K // 2, 128), F32)),
        in_specs=[hbm, hbm, hbm],
        out_specs=(vmem, vmem),
        scratch_shapes=[
            pltpu.VMEM((STATIONS, fn, fn), BF),
            pltpu.VMEM((2, STATIONS, fn, fn), BF),
            pltpu.VMEM((STATIONS, fn), F32),
            pltpu.VMEM((2, 2 * STATIONS, fn), F32),
            pltpu.VMEM((fn, lz * K), BF),
            pltpu.VMEM((CHUNKS, rows, fn), BF),
            pltpu.VMEM((CHUNKS, rows, fn), BF),
            pltpu.VMEM((CHUNKS, 2 * half + rows, fn), BF),
            pltpu.VMEM((CHUNKS, 3 * rows, fn), BF),
            pltpu.VMEM((CHUNKS, rows, fn), BF),
            pltpu.VMEM((3 * rows, fn), BF),
            pltpu.VMEM((3 * rows, fn), BF),
            pltpu.VMEM((2, CHUNKS, rows, fn), BF),
            pltpu.VMEM((2, CHUNKS, rows, fn), BF),
            pltpu.VMEM((ny, K // 2, 128), F32),
            pltpu.VMEM((nz, K // 2, 128), F32),
            dma((STATIONS + 2,)),
            dma((STATIONS,)), dma((STATIONS,)),
            dma((1,)), dma((1,)),
            dma((CHUNKS,)), dma((CHUNKS,)),
            dma((CHUNKS, 2)), dma((CHUNKS, 2)),
            dma((CHUNKS,)), dma((CHUNKS,)),
            dma((CHUNKS, 2)), dma((CHUNKS, 2)),
            dma((CHUNKS,)), dma((CHUNKS,)),
            dma((ny - 1,)), dma((ny - 1,)),
            dma((nz - 1,)), dma((nz - 1,)),
        ],
        compiler_params=pltpu.CompilerParams(collective_id=0, has_side_effects=True, vmem_limit_bytes=60 << 20),
    )(inverse_blocks, coupling, sources[0])
    basis, upper = pl.pallas_call(
        functools.partial(basis_kernel, lz, count),
        name="basis",
        out_shape=(jax.ShapeDtypeStruct((fn, lz * K), BF), jax.ShapeDtypeStruct((K, K), F32)),
        in_specs=[vmem, vmem],
        out_specs=(vmem, vmem),
        compiler_params=pltpu.CompilerParams(vmem_limit_bytes=48 << 20),
    )(yt, gram)
    return basis[None], upper[None]


def solution(mesh):
    placed = (P("section", None, None), P("section", None), P("section", None, "span"))
    sizes = grid_sizes(mesh)

    def whole(inverse_blocks, coupling, sources):
        count = float(sources.shape[1] * sources.shape[2] // K)
        return jax.shard_map(
            functools.partial(local, sizes, count),
            mesh=mesh,
            in_specs=placed,
            out_specs=(P("section", None, "span"), P("section", None, None)),
            check_vma=False,
        )(inverse_blocks, coupling, sources)

    return whole
```

time: 107 us -> 87 us (0.81)
  Pallas kernels: 102 us -> 84.4 us
  local copies, waits for them, and re-layouts: 4.1 us -> 1.76 us
    pallas_call x1, Pallas kernels: 95.8 us -> 78.5 us  [local(): pl.pallas_call(functools.partial(march_kernel, sizes, lz, fn), name='marc...]
    unnamed x6 -> x4, local copies, waits for them, and re-layouts: 4.1 us -> 1.76 us
where the time goes in v2:
time: 87 us; the launch traced here: 86.8 us
  Pallas kernels  84.4 us (97%)
  local copies, waits for them, and re-layouts  1.76 us (2%)
    pallas_call x1, Pallas kernels, local(): pl.pallas_call(functools.partial(march_kernel, sizes, lz, fn), name='marc...  78.5 us
    pallas_call x1, Pallas kernels, local(): pl.pallas_call(functools.partial(basis_kernel, lz, count), name='basis',...  5.91 us
    unnamed x4, local copies, waits for them, and re-layouts  1.76 us

profile of v2, /device:TPU:32, one launch (start us, length us, event | category | flops | bytes accessed | tf_op | source)
XLA Modules:
  0.0 86.8 jit_solution(10046939304174799410)
XLA Ops:
  0.6 78.5 %march.1 = (bf16[768,384]{1,0:T(8,128)(2,1)}, f32[24,128]{1,0:T(8,128)}) custom-call(bf16[4,768,768]{2,1,0:T(8,128)(2,1)} %a_hbm.1, f32[4,768]{1,0:T(4,128)} %c_hbm.1, bf16[768,384]{1,0:T(8,128)(2,1)} %bitcast.3), custom_call_target="tpu_custom_call" | custom-call | tf_op jit(solution)/shard_map/march/pallas_call | solution.py:333
  79.1 0.0 copy-start
  79.1 1.1 %copy-done = bf16[768,384]{1,0:T(8,128)(2,1)S(1)} copy-done((bf16[768,384]{1,0:T(8,128)(2,1)S(1)}, bf16[768,384]{1,0:T(8,128)(2,1)}, u32[]{:S(2)}) %copy-start) | copy-done | bytes 589848
  80.2 0.0 copy-start.1
  80.2 0.7 copy-done.1
  80.9 5.9 %basis.1 = (bf16[768,384]{1,0:T(8,128)(2,1)}, f32[48,48]{1,0:T(8,128)}) custom-call(bf16[768,384]{1,0:T(8,128)(2,1)S(1)} %copy-done, f32[24,128]{1,0:T(8,128)S(1)} %copy-done.1), custom_call_target="tpu_custom_call" | custom-call | tf_op jit(solution)/shard_map/basis/pallas_call | solution.py:369
Async XLA Ops:
  79.1 1.1 %copy-start = (bf16[768,384]{1,0:T(8,128)(2,1)S(1)}, bf16[768,384]{1,0:T(8,128)(2,1)}, u32[]{:S(2)}) copy-start(bf16[768,384]{1,0:T(8,128)(2,1)} %get-tuple-element.6.yt_ref) | copy-start | bytes 1769476
  80.2 0.7 copy-start.1

commit v3 on v2

--- a/solution.py
+++ b/solution.py
@@ -12,6 +12,8 @@
 STATIONS = 4
 KC = 8
 CHUNKS = 3
+PIECES = 3
+BLOCK = 8
 BF = jnp.bfloat16
 F32 = jnp.float32
 
@@ -22,7 +24,7 @@
     return mesh.shape["section"], rows, span // rows
 
 
-def march_kernel(sizes, lz, fn, a_hbm, c_hbm, s_hbm, yt_ref, g_ref,
+def march_kernel(sizes, lz, fn, count, a_hbm, c_hbm, s_hbm, yt, w_ref,
                  av, at, cv, cc, sv, tmp, sa, sb, ext, inc, wa, wb, ym, yf, gy, gz,
                  lsem, wsend, wrecv, csend, crecv, ssend, srecv, bsend, brecv,
                  msend, mrecv, hsend, hrecv, xsend, xrecv, ysend, yrecv, zsend, zrecv):
@@ -75,13 +77,20 @@
     middle = pl.ds(half, rows)
     source_cross_a = lambda j: remote(tmp.at[j], sa.at[j], ssend.at[j], srecv.at[j], other)
     source_cross_b = lambda j: remote(tmp.at[j], sb.at[j, middle], ssend.at[j], srecv.at[j], other)
-    main_copy = lambda j: remote(ym.at[0, j], inc.at[j], msend.at[j], mrecv.at[j], below)
+    width = fn // PIECES
+    lanes = lambda p: pl.ds(p * width, width)
+    everything = pl.ds(0, rows)
+
+    def main_copy(j, p):
+        return remote(ym.at[0, j, everything, lanes(p)], inc.at[j, everything, lanes(p)],
+                      msend.at[j, p], mrecv.at[j, p], below)
+
     cross_y = lambda j: remote(ym.at[1 - core, j], yf.at[core, j], xsend.at[j], xrecv.at[j], other)
 
-    def halo_copy(j, side):
+    def halo_copy(j, side, p):
         target, device = ((2 * rows, left), (0, right))[side]
-        return remote(ext.at[j, pl.ds(rows, rows)], ext.at[j, pl.ds(target, rows)],
-                      hsend.at[j, side], hrecv.at[j, side], device)
+        return remote(ext.at[j, pl.ds(rows, rows), lanes(p)], ext.at[j, pl.ds(target, rows), lanes(p)],
+                      hsend.at[j, side, p], hrecv.at[j, side, p], device)
 
     def source_halo(j, side):
         start, target, device = ((half, half + rows, left), (rows, 0, right))[side]
@@ -89,25 +98,25 @@
                       bsend.at[j, side], brecv.at[j, side], device)
 
     source_copy.wait()
-    wide_row = lax.broadcasted_iota(jnp.int32, (rows, lz * K), 0)
-    wide_lane = lax.broadcasted_iota(jnp.int32, (rows, lz * K), 1)
-    base_lane = (wide_row // KC) * K + lax.rem(wide_row, KC)
-
-    def columns(h, j):
-        pick = (wide_lane == base_lane + (h * (K // 2) + j * KC)).astype(F32).astype(BF)
-        return lax.dot_general(pick, sv[...], (((1,), (1,)), ((), ())), preferred_element_type=F32).astype(BF)
-
-    for j in range(CHUNKS):
-        tmp[j] = columns(1 - core, j)
-        mine = columns(core, j)
-
-        @pl.when(is_one)
-        def _():
-            sa[j] = mine
-
-        @pl.when(is_zero)
-        def _():
-            sb[j, middle, :] = mine
+    total = 2 * CHUNKS * rows
+    pick_row = lax.broadcasted_iota(jnp.int32, (total, lz * K), 0)
+    pick_lane = lax.broadcasted_iota(jnp.int32, (total, lz * K), 1)
+    in_half = lax.rem(pick_row, CHUNKS * rows)
+    owner = jnp.where(pick_row < CHUNKS * rows, core, 1 - core)
+    in_chunk = lax.rem(in_half, rows)
+    source_lane = (in_chunk // KC) * K + owner * (K // 2) + (in_half // rows) * KC + lax.rem(in_chunk, KC)
+    pick = (pick_lane == source_lane).astype(F32).astype(BF)
+    moved = lax.dot_general(pick, sv[...], (((1,), (1,)), ((), ())), preferred_element_type=F32).astype(BF)
+    mine = moved[:CHUNKS * rows].reshape(CHUNKS, rows, fn)
+    tmp[...] = moved[CHUNKS * rows:].reshape(CHUNKS, rows, fn)
+
+    @pl.when(is_one)
+    def _():
+        sa[...] = mine
+
+    @pl.when(is_zero)
+    def _():
+        sb[:, middle, :] = mine
 
     rate_copy.wait()
     cc[core] = jnp.concatenate([cv[...], jnp.zeros_like(cv)], axis=0)
@@ -132,8 +141,9 @@
                 source_cross_a(j).wait_recv()
 
             ext[j, pl.ds(rows, rows), :] = sa[j]
-            halo_copy(j, 0).start()
-            halo_copy(j, 1).start()
+            for p in range(PIECES):
+                halo_copy(j, 0, p).start()
+                halo_copy(j, 1, p).start()
 
     for i in reversed(range(STATIONS)):
         weight_copies[i].wait()
@@ -157,12 +167,14 @@
     def prepare(j):
         @pl.when(jnp.logical_not(first_chip))
         def _():
-            main_copy(j).wait_recv()
-            ext[j, pl.ds(rows, rows), :] = (inc[j].astype(F32) + sa[j].astype(F32)).astype(BF)
-            halo_copy(j, 0).start()
-            halo_copy(j, 1).start()
-
-    def station(j, p, i, value):
+            for p in range(PIECES):
+                main_copy(j, p).wait_recv()
+                at_piece = (j, everything, lanes(p))
+                ext[j, pl.ds(rows, rows), lanes(p)] = (inc[at_piece].astype(F32) + sa[at_piece].astype(F32)).astype(BF)
+                halo_copy(j, 0, p).start()
+                halo_copy(j, 1, p).start()
+
+    def diffuse(j, p, i, value):
         @pl.when(jnp.logical_and(j == 0, core != p))
         def _():
             weight_cross(p, i).wait_recv()
@@ -170,14 +182,17 @@
         w = value.astype(F32)
         center = w[KC:-KC]
         spread = w[2 * KC:] + w[:-2 * KC] - 2.0 * center
-        update = (center + cc[p, i:i + 1, :] * spread).astype(BF)
-        return jnp.dot(update, at[p, i], preferred_element_type=F32).astype(BF)
+        return (center + cc[p, i:i + 1, :] * spread).astype(BF)
+
+    def station(j, p, i, value):
+        return jnp.dot(diffuse(j, p, i, value), at[p, i], preferred_element_type=F32).astype(BF)
 
     def compute(j):
         n = 3 * rows
         step = 2 * KC
-        halo_copy(j, 0).wait_recv()
-        halo_copy(j, 1).wait_recv()
+        for p in range(PIECES):
+            halo_copy(j, 0, p).wait_recv()
+            halo_copy(j, 1, p).wait_recv()
         wa[pl.ds(0, n - step), :] = station(j, 1, 3, ext[j])
         wb[pl.ds(0, n - 2 * step), :] = station(j, 1, 2, wa[pl.ds(0, n - step), :])
         wa[pl.ds(0, n - 3 * step), :] = station(j, 1, 1, wb[pl.ds(0, n - 2 * step), :])
@@ -200,11 +215,14 @@
         wa[pl.ds(0, n - step), :] = station(j, 0, 3, value)
         wb[pl.ds(0, n - 2 * step), :] = station(j, 0, 2, wa[pl.ds(0, n - step), :])
         wa[pl.ds(0, n - 3 * step), :] = station(j, 0, 1, wb[pl.ds(0, n - 2 * step), :])
-        ym[0, j] = station(j, 0, 0, wa[pl.ds(0, n - 3 * step), :])
-
-        @pl.when(jnp.logical_not(last_chip))
-        def _():
-            main_copy(j).start()
+        update = diffuse(j, 0, 0, wa[pl.ds(0, n - 3 * step), :])
+        for p in range(PIECES):
+            ym[0, j, everything, lanes(p)] = jnp.dot(
+                update, at[0, 0, :, lanes(p)], preferred_element_type=F32).astype(BF)
+
+            @pl.when(jnp.logical_not(last_chip))
+            def _():
+                main_copy(j, p).start()
 
         @pl.when(is_zero)
         def _():
@@ -228,7 +246,6 @@
     for j in range(CHUNKS):
         cross_y(j).wait_recv()
 
-    total = 2 * CHUNKS * rows
     flat = yf[...].reshape(total, fn)
     gram = lax.dot_general(flat, flat, (((1,), (1,)), ((), ())), preferred_element_type=F32)
     z_of_row = lax.rem(lax.broadcasted_iota(jnp.int32, (total, total), 0), rows) // KC
@@ -250,7 +267,7 @@
 
     for d in range(1, ny):
         y_copy(d).start()
-    yt_ref[...] = flat.T
+    yt[...] = flat.T
     for d in range(1, ny):
         y_copy(d).wait_recv()
     acc = gy[0]
@@ -264,7 +281,6 @@
     acc = gz[0]
     for i in range(1, nz):
         acc = acc + gz[i]
-    g_ref[...] = acc
 
     rate_cross(core).wait_send()
     for i in range(STATIONS):
@@ -272,37 +288,46 @@
     for j in range(CHUNKS):
         source_cross_a(j).wait_send()
         for side in (0, 1):
-            halo_copy(j, side).wait_send()
+            for p in range(PIECES):
+                halo_copy(j, side, p).wait_send()
             source_halo(j, side).wait_send()
         cross_y(j).wait_send()
 
         @pl.when(jnp.logical_not(last_chip))
         def _():
-            main_copy(j).wait_send()
+            for p in range(PIECES):
+                main_copy(j, p).wait_send()
 
     for d in range(1, ny):
         y_copy(d).wait_send()
     for d in range(1, nz):
         z_copy(d).wait_send()
 
-
-def basis_kernel(lz, count, yt_ref, g_ref, o_ref, u_ref):
+    row = lax.broadcasted_iota(jnp.int32, (K, 128), 0)
+    scaled = jnp.concatenate([acc, pltpu.roll(acc, 64, 1)], axis=0) * (1.0 / count)
+    w = jnp.where(lane < K, scaled, jnp.where(lane == row + 64, 1.0, 0.0))
+    for start in range(0, K, BLOCK):
+        columns = [jnp.broadcast_to(w[:, start + b:start + b + 1], (K, 128)) for b in range(BLOCK)]
+        for b in range(BLOCK):
+            j = start + b
+            inverse = lax.rsqrt(columns[b][j:j + 1, :])
+            unit = w[j:j + 1, :] * inverse
+            column = jnp.where(row > j, columns[b] * inverse, 0.0)
+            for later in range(b + 1, BLOCK):
+                columns[later] = columns[later] - column * (columns[later][j:j + 1, :] * inverse)
+            w = jnp.where(row == j, unit, w - column * unit)
+    w_ref[...] = w
+
+
+def basis_kernel(lz, yt, w_ref, o_ref, u_ref):
     rows = lz * KC
+    w = w_ref[...]
     lane = lax.broadcasted_iota(jnp.int32, (K, 128), 1)
     row = lax.broadcasted_iota(jnp.int32, (K, 128), 0)
-    gram = jnp.concatenate([g_ref[...], pltpu.roll(g_ref[...], 64, 1)], axis=0)
-    scaled = gram * (1.0 / count)
-    w = jnp.where(lane < K, scaled, jnp.where(lane == row + 64, 1.0, 0.0))
-    for j in range(K):
-        pivot = w[j:j + 1, :]
-        inv = lax.rsqrt(w[j:j + 1, j:j + 1])
-        unit = pivot * inv
-        column = w[:, j:j + 1] * inv
-        w = jnp.where(row == j, unit, w - jnp.where(row > j, column, 0.0) * unit)
     u_ref[...] = jnp.where(lane >= row, w, 0.0)[:, :K]
     tile_row = lax.broadcasted_iota(jnp.int32, (K, lz * K), 0)
     tile_lane = lax.broadcasted_iota(jnp.int32, (K, lz * K), 1)
-    spread = (tile_row == lax.rem(tile_lane, K)).astype(F32).astype(BF)
+    copies = (tile_row == lax.rem(tile_lane, K)).astype(F32).astype(BF)
     high = w.astype(BF)
     low = (w - high.astype(F32)).astype(BF)
     block_row = lax.broadcasted_iota(jnp.int32, (rows, lz * K), 0)
@@ -310,13 +335,13 @@
     same = block_row // KC == block_lane // K
     out = None
     for part in (high, low):
-        tiled = lax.dot_general(part, spread, (((0,), (0,)), ((), ())), preferred_element_type=F32)
+        tiled = lax.dot_general(part, copies, (((0,), (0,)), ((), ())), preferred_element_type=F32)
         blocks = []
         for c in range(2 * CHUNKS):
             one = tiled[64 + c * KC:64 + (c + 1) * KC]
             blocks.append(jnp.where(same, jnp.concatenate([one] * lz, axis=0), 0.0))
         block = jnp.concatenate(blocks, axis=0).astype(BF)
-        term = jnp.dot(yt_ref[...], block, preferred_element_type=F32)
+        term = jnp.dot(yt[...], block, preferred_element_type=F32)
         out = term if out is None else out + term
     o_ref[...] = out.astype(BF)
 
@@ -330,10 +355,10 @@
     hbm = pl.BlockSpec(memory_space=pltpu.HBM)
     vmem = pl.BlockSpec(memory_space=pltpu.VMEM)
     dma = pltpu.SemaphoreType.DMA
-    yt, gram = pl.pallas_call(
-        functools.partial(march_kernel, sizes, lz, fn),
+    yt, factors = pl.pallas_call(
+        functools.partial(march_kernel, sizes, lz, fn, count),
         name="march",
-        out_shape=(jax.ShapeDtypeStruct((fn, lz * K), BF), jax.ShapeDtypeStruct((K // 2, 128), F32)),
+        out_shape=(pltpu.VMEM((fn, lz * K), BF), pltpu.VMEM((K, 128), F32)),
         in_specs=[hbm, hbm, hbm],
         out_specs=(vmem, vmem),
         scratch_shapes=[
@@ -358,8 +383,8 @@
             dma((1,)), dma((1,)),
             dma((CHUNKS,)), dma((CHUNKS,)),
             dma((CHUNKS, 2)), dma((CHUNKS, 2)),
-            dma((CHUNKS,)), dma((CHUNKS,)),
-            dma((CHUNKS, 2)), dma((CHUNKS, 2)),
+            dma((CHUNKS, PIECES)), dma((CHUNKS, PIECES)),
+            dma((CHUNKS, 2, PIECES)), dma((CHUNKS, 2, PIECES)),
             dma((CHUNKS,)), dma((CHUNKS,)),
             dma((ny - 1,)), dma((ny - 1,)),
             dma((nz - 1,)), dma((nz - 1,)),
@@ -367,13 +392,13 @@
         compiler_params=pltpu.CompilerParams(collective_id=0, has_side_effects=True, vmem_limit_bytes=60 << 20),
     )(inverse_blocks, coupling, sources[0])
     basis, upper = pl.pallas_call(
-        functools.partial(basis_kernel, lz, count),
+        functools.partial(basis_kernel, lz),
         name="basis",
         out_shape=(jax.ShapeDtypeStruct((fn, lz * K), BF), jax.ShapeDtypeStruct((K, K), F32)),
         in_specs=[vmem, vmem],
         out_specs=(vmem, vmem),
-        compiler_params=pltpu.CompilerParams(vmem_limit_bytes=48 << 20),
-    )(yt, gram)
+        compiler_params=pltpu.CompilerParams(vmem_limit_bytes=32 << 20),
+    )(yt, factors)
     return basis[None], upper[None]
 
 

time: 87 us -> 79 us (0.908)
  Pallas kernels: 84.4 us -> 78.3 us
  local copies, waits for them, and re-layouts: 1.76 us -> 0 us
    pallas_call x2, Pallas kernels: 84.4 us -> 78.3 us  [the longest x1 76.3 us: local(): pl.pallas_call(functools.partial(march_kernel, sizes, lz, fn, count), nam...]
    unnamed x4 -> x0, local copies, waits for them, and re-layouts: 1.76 us -> none
where the time goes in v3:
time: 79 us; the launch traced here: 78.9 us
  Pallas kernels  78.3 us (99%)
    pallas_call x1, Pallas kernels, local(): pl.pallas_call(functools.partial(march_kernel, sizes, lz, fn, count), nam...  76.3 us
    pallas_call x1, Pallas kernels, local(): pl.pallas_call(functools.partial(basis_kernel, lz), name='basis', out_sha...  1.92 us

profile of v3, /device:TPU:32, one launch (start us, length us, event | category | flops | bytes accessed | tf_op | source)
XLA Modules:
  0.0 78.9 jit_solution(78097202950883738)
XLA Ops:
  0.6 76.3 %march.1 = (bf16[768,384]{1,0:T(8,128)(2,1)S(1)}, f32[48,128]{1,0:T(8,128)S(1)}) custom-call(bf16[4,768,768]{2,1,0:T(8,128)(2,1)} %a_hbm.1, f32[4,768]{1,0:T(4,128)} %c_hbm.1, bf16[768,384]{1,0:T(8,128)(2,1)} %bitcast.3), custom_call_target="tpu_custom_call" | custom-call | tf_op jit(solution)/shard_map/march/pallas_call | solution.py:358
  77.0 1.9 %basis.1 = (bf16[768,384]{1,0:T(8,128)(2,1)}, f32[48,48]{1,0:T(8,128)}) custom-call(bf16[768,384]{1,0:T(8,128)(2,1)S(1)} %get-tuple-element.6.yt, f32[48,128]{1,0:T(8,128)S(1)} %get-tuple-element.7.w_ref), custom_call_target="tpu_custom_call" | custom-call | tf_op jit(solution)/shard_map/basis/pallas_call | solution.py:394

commit v4 on v3

--- a/solution.py
+++ b/solution.py
@@ -25,7 +25,7 @@
 
 
 def march_kernel(sizes, lz, fn, count, a_hbm, c_hbm, s_hbm, yt, w_ref,
-                 av, at, cv, cc, sv, tmp, sa, sb, ext, inc, wa, wb, ym, yf, gy, gz,
+                 av, aw, at, cv, cc, sv, tmp, sa, sb, ext, inc, wa, wb, ym, yf, gy, gz,
                  lsem, wsend, wrecv, csend, crecv, ssend, srecv, bsend, brecv,
                  msend, mrecv, hsend, hrecv, xsend, xrecv, ysend, yrecv, zsend, zrecv):
     ng, ny, nz = sizes
@@ -72,7 +72,7 @@
         return pltpu.make_async_remote_copy(
             src_ref=src, dst_ref=dst, send_sem=send, recv_sem=recv, device_id=device, device_id_type=MESH)
 
-    weight_cross = lambda p, i: remote(at.at[p, i], at.at[p, i], wsend.at[i], wrecv.at[i], other)
+    weight_cross = lambda i: remote(a_hbm.at[i], aw.at[i], wsend.at[i], wrecv.at[i], other)
     rate_cross = lambda p: remote(cc.at[p], cc.at[p], csend.at[0], crecv.at[0], other)
     middle = pl.ds(half, rows)
     source_cross_a = lambda j: remote(tmp.at[j], sa.at[j], ssend.at[j], srecv.at[j], other)
@@ -99,16 +99,32 @@
 
     source_copy.wait()
     total = 2 * CHUNKS * rows
-    pick_row = lax.broadcasted_iota(jnp.int32, (total, lz * K), 0)
-    pick_lane = lax.broadcasted_iota(jnp.int32, (total, lz * K), 1)
-    in_half = lax.rem(pick_row, CHUNKS * rows)
-    owner = jnp.where(pick_row < CHUNKS * rows, core, 1 - core)
-    in_chunk = lax.rem(in_half, rows)
-    source_lane = (in_chunk // KC) * K + owner * (K // 2) + (in_half // rows) * KC + lax.rem(in_chunk, KC)
-    pick = (pick_lane == source_lane).astype(F32).astype(BF)
-    moved = lax.dot_general(pick, sv[...], (((1,), (1,)), ((), ())), preferred_element_type=F32).astype(BF)
-    mine = moved[:CHUNKS * rows].reshape(CHUNKS, rows, fn)
-    tmp[...] = moved[CHUNKS * rows:].reshape(CHUNKS, rows, fn)
+    pick_row = lax.broadcasted_iota(jnp.int32, (CHUNKS * rows, lz * K), 0)
+    pick_lane = lax.broadcasted_iota(jnp.int32, (CHUNKS * rows, lz * K), 1)
+    in_chunk = lax.rem(pick_row, rows)
+    source_lane = (in_chunk // KC) * K + (pick_row // rows) * KC + lax.rem(in_chunk, KC)
+
+    def columns(h):
+        pick = (pick_lane == source_lane + h * (K // 2)).astype(F32).astype(BF)
+        moved = lax.dot_general(pick, sv[...], (((1,), (1,)), ((), ())), preferred_element_type=F32)
+        return moved.astype(BF).reshape(CHUNKS, rows, fn)
+
+    tmp[...] = columns(1 - core)
+    pl.semaphore_wait(barrier, ny + nz + 3)
+
+    for j in range(CHUNKS):
+        @pl.when(is_one)
+        def _():
+            source_cross_a(j).start()
+
+        @pl.when(is_zero)
+        def _():
+            source_cross_b(j).start()
+
+        weight_cross(STATIONS - 1 - j).start()
+    for i in reversed(range(STATIONS - CHUNKS)):
+        weight_cross(i).start()
+    mine = columns(core)
 
     @pl.when(is_one)
     def _():
@@ -118,24 +134,9 @@
     def _():
         sb[:, middle, :] = mine
 
-    rate_copy.wait()
-    cc[core] = jnp.concatenate([cv[...], jnp.zeros_like(cv)], axis=0)
-    pl.semaphore_wait(barrier, ny + nz + 3)
-
-    for j in range(CHUNKS):
-        @pl.when(is_one)
-        def _():
-            source_cross_a(j).start()
-
-        @pl.when(is_zero)
-        def _():
-            source_cross_b(j).start()
-
-    rate_cross(core).start()
-
-    @pl.when(first_chip)
-    def _():
-        for j in range(CHUNKS):
+    def begin(j):
+        @pl.when(first_chip)
+        def _():
             @pl.when(is_zero)
             def _():
                 source_cross_a(j).wait_recv()
@@ -145,24 +146,42 @@
                 halo_copy(j, 0, p).start()
                 halo_copy(j, 1, p).start()
 
+    def share_sources(j):
+        @pl.when(is_one)
+        def _():
+            source_cross_b(j).wait_recv()
+
+        @pl.when(jnp.logical_and(is_zero, jnp.logical_not(first_chip)))
+        def _():
+            source_cross_a(j).wait_recv()
+
+        source_halo(j, 0).start()
+        source_halo(j, 1).start()
+
+    begin(0)
+    share_sources(0)
+    rate_copy.wait()
+    cc[core] = jnp.concatenate([cv[...], jnp.zeros_like(cv)], axis=0)
+    rate_cross(core).start()
     for i in reversed(range(STATIONS)):
         weight_copies[i].wait()
         at[core, i] = av[i].T
-        weight_cross(core, i).start()
-
-    for j in range(CHUNKS):
-        @pl.when(is_one)
-        def _():
-            source_cross_b(j).wait_recv()
-
-        @pl.when(jnp.logical_and(is_zero, jnp.logical_not(first_chip)))
-        def _():
-            source_cross_a(j).wait_recv()
-
-        source_halo(j, 0).start()
-        source_halo(j, 1).start()
+        if i == STATIONS // 2:
+            begin(1)
+            share_sources(1)
+    begin(2)
+    share_sources(2)
 
     rate_cross(1 - core).wait_recv()
+
+    def receive_weights(i):
+        weight_cross(i).wait_recv()
+        at[1 - core, i] = aw[i].T
+
+    @pl.when(jnp.logical_not(first_chip))
+    def _():
+        for i in reversed(range(STATIONS)):
+            receive_weights(i)
 
     def prepare(j):
         @pl.when(jnp.logical_not(first_chip))
@@ -174,15 +193,20 @@
                 halo_copy(j, 0, p).start()
                 halo_copy(j, 1, p).start()
 
-    def diffuse(j, p, i, value):
-        @pl.when(jnp.logical_and(j == 0, core != p))
-        def _():
-            weight_cross(p, i).wait_recv()
-
+    def arrive(j, p, i):
+        @pl.when(jnp.logical_and(jnp.logical_and(j == 0, first_chip), core != p))
+        def _():
+            receive_weights(i)
+
+    def spread_out(value, rates):
         w = value.astype(F32)
         center = w[KC:-KC]
         spread = w[2 * KC:] + w[:-2 * KC] - 2.0 * center
-        return (center + cc[p, i:i + 1, :] * spread).astype(BF)
+        return (center + rates * spread).astype(BF)
+
+    def diffuse(j, p, i, value):
+        arrive(j, p, i)
+        return spread_out(value, cc[p, i:i + 1, :])
 
     def station(j, p, i, value):
         return jnp.dot(diffuse(j, p, i, value), at[p, i], preferred_element_type=F32).astype(BF)
@@ -190,10 +214,16 @@
     def compute(j):
         n = 3 * rows
         step = 2 * KC
+        product = None
         for p in range(PIECES):
             halo_copy(j, 0, p).wait_recv()
             halo_copy(j, 1, p).wait_recv()
-        wa[pl.ds(0, n - step), :] = station(j, 1, 3, ext[j])
+            if p == 0:
+                arrive(j, 1, 3)
+            update = spread_out(ext[j, :, lanes(p)], cc[1, 3:4, lanes(p)])
+            term = jnp.dot(update, at[1, 3, lanes(p), :], preferred_element_type=F32)
+            product = term if product is None else product + term
+        wa[pl.ds(0, n - step), :] = product.astype(BF)
         wb[pl.ds(0, n - 2 * step), :] = station(j, 1, 2, wa[pl.ds(0, n - step), :])
         wa[pl.ds(0, n - 3 * step), :] = station(j, 1, 1, wb[pl.ds(0, n - 2 * step), :])
         n = 2 * rows
@@ -214,6 +244,11 @@
         value = (upper_out.astype(F32) + sb[j].astype(F32)).astype(BF)
         wa[pl.ds(0, n - step), :] = station(j, 0, 3, value)
         wb[pl.ds(0, n - 2 * step), :] = station(j, 0, 2, wa[pl.ds(0, n - step), :])
+
+        @pl.when(j < CHUNKS - 2)
+        def _():
+            prepare(j + 2)
+
         wa[pl.ds(0, n - 3 * step), :] = station(j, 0, 1, wb[pl.ds(0, n - 2 * step), :])
         update = diffuse(j, 0, 0, wa[pl.ds(0, n - 3 * step), :])
         for p in range(PIECES):
@@ -233,12 +268,9 @@
             cross_y(j).start()
 
     prepare(0)
+    prepare(1)
 
     def chunk_step(j, carry):
-        @pl.when(j < CHUNKS - 1)
-        def _():
-            prepare(j + 1)
-
         compute(j)
         return carry
 
@@ -260,7 +292,10 @@
         for shift in (64, 32, 16, 8):
             tile = tile + pltpu.roll(tile, shift, 1)
         packed = jnp.where(lane // KC == c, tile, packed)
-    gy[my] = packed[:K // 2] + pltpu.roll(packed[K // 2:], 64, 1)
+    first, second, third = packed[:16], packed[16:32], packed[32:]
+    top = lax.broadcasted_iota(jnp.int32, (16, 128), 1)
+    sides = jnp.where(top < 64, pltpu.roll(third, 16, 1), pltpu.roll(second, 48, 1))
+    gy[my] = jnp.where(top < K, first, jnp.where(top < 96, sides, 0.0))
 
     y_copy = lambda d: remote(gy.at[my], gy.at[my], ysend.at[d - 1], yrecv.at[d - 1], y_peer(d))
     z_copy = lambda d: remote(gz.at[mz], gz.at[mz], zsend.at[d - 1], zrecv.at[d - 1], z_peer(d))
@@ -284,7 +319,7 @@
 
     rate_cross(core).wait_send()
     for i in range(STATIONS):
-        weight_cross(core, i).wait_send()
+        weight_cross(i).wait_send()
     for j in range(CHUNKS):
         source_cross_a(j).wait_send()
         for side in (0, 1):
@@ -304,8 +339,10 @@
         z_copy(d).wait_send()
 
     row = lax.broadcasted_iota(jnp.int32, (K, 128), 0)
-    scaled = jnp.concatenate([acc, pltpu.roll(acc, 64, 1)], axis=0) * (1.0 / count)
-    w = jnp.where(lane < K, scaled, jnp.where(lane == row + 64, 1.0, 0.0))
+    scaled = jnp.concatenate([acc, pltpu.roll(acc, 80, 1), pltpu.roll(acc, 112, 1)], axis=0) * (1.0 / count)
+    upper = jnp.where(jnp.logical_and(lane < K, lane >= row), scaled, 0.0)
+    lower = jnp.concatenate([upper, jnp.zeros((128 - K, 128), F32)], axis=0).T[:K]
+    w = jnp.where(lane > row, upper, lower) + jnp.where(lane == row + 64, 1.0, 0.0)
     for start in range(0, K, BLOCK):
         columns = [jnp.broadcast_to(w[:, start + b:start + b + 1], (K, 128)) for b in range(BLOCK)]
         for b in range(BLOCK):
@@ -363,6 +400,7 @@
         out_specs=(vmem, vmem),
         scratch_shapes=[
             pltpu.VMEM((STATIONS, fn, fn), BF),
+            pltpu.VMEM((STATIONS, fn, fn), BF),
             pltpu.VMEM((2, STATIONS, fn, fn), BF),
             pltpu.VMEM((STATIONS, fn), F32),
             pltpu.VMEM((2, 2 * STATIONS, fn), F32),
@@ -376,8 +414,8 @@
             pltpu.VMEM((3 * rows, fn), BF),
             pltpu.VMEM((2, CHUNKS, rows, fn), BF),
             pltpu.VMEM((2, CHUNKS, rows, fn), BF),
-            pltpu.VMEM((ny, K // 2, 128), F32),
-            pltpu.VMEM((nz, K // 2, 128), F32),
+            pltpu.VMEM((ny, K // 3, 128), F32),
+            pltpu.VMEM((nz, K // 3, 128), F32),
             dma((STATIONS + 2,)),
             dma((STATIONS,)), dma((STATIONS,)),
             dma((1,)), dma((1,)),

time: 79 us -> 75.8 us (0.959)
  Pallas kernels: 78.3 us -> 75.1 us
    pallas_call x1, Pallas kernels: 76.3 us -> 73.2 us  [local(): pl.pallas_call(functools.partial(march_kernel, sizes, lz, fn, count), nam...]
where the time goes in v4:
time: 75.8 us
  Pallas kernels  75.1 us (99%)
    pallas_call x1, Pallas kernels, local(): pl.pallas_call(functools.partial(march_kernel, sizes, lz, fn, count), nam...  73.2 us
    pallas_call x1, Pallas kernels, local(): pl.pallas_call(functools.partial(basis_kernel, lz), name='basis', out_sha...  1.92 us

profile of v4, /device:TPU:32, one launch (start us, length us, event | category | flops | bytes accessed | tf_op | source)
XLA Modules:
  0.0 75.8 jit_solution(15002480885840087598)
XLA Ops:
  0.6 73.2 %march.1 = (bf16[768,384]{1,0:T(8,128)(2,1)S(1)}, f32[48,128]{1,0:T(8,128)S(1)}) custom-call(bf16[4,768,768]{2,1,0:T(8,128)(2,1)} %a_hbm.1, f32[4,768]{1,0:T(4,128)} %c_hbm.1, bf16[768,384]{1,0:T(8,128)(2,1)} %bitcast.3), custom_call_target="tpu_custom_call" | custom-call | tf_op jit(solution)/shard_map/march/pallas_call | solution.py:395
  73.8 1.9 %basis.1 = (bf16[768,384]{1,0:T(8,128)(2,1)}, f32[48,48]{1,0:T(8,128)}) custom-call(bf16[768,384]{1,0:T(8,128)(2,1)S(1)} %get-tuple-element.6.yt, f32[48,128]{1,0:T(8,128)S(1)} %get-tuple-element.7.w_ref), custom_call_target="tpu_custom_call" | custom-call | tf_op jit(solution)/shard_map/basis/pallas_call | solution.py:432

commit v5 on v4

--- a/solution.py
+++ b/solution.py
@@ -72,7 +72,13 @@
         return pltpu.make_async_remote_copy(
             src_ref=src, dst_ref=dst, send_sem=send, recv_sem=recv, device_id=device, device_id_type=MESH)
 
-    weight_cross = lambda i: remote(a_hbm.at[i], aw.at[i], wsend.at[i], wrecv.at[i], other)
+    early = STATIONS // 2
+
+    def weight_cross(p, i):
+        if i >= early:
+            return remote(a_hbm.at[i], aw.at[i - early], wsend.at[i], wrecv.at[i], other)
+        return remote(at.at[p, i], at.at[p, i], wsend.at[i], wrecv.at[i], other)
+
     rate_cross = lambda p: remote(cc.at[p], cc.at[p], csend.at[0], crecv.at[0], other)
     middle = pl.ds(half, rows)
     source_cross_a = lambda j: remote(tmp.at[j], sa.at[j], ssend.at[j], srecv.at[j], other)
@@ -121,9 +127,8 @@
         def _():
             source_cross_b(j).start()
 
-        weight_cross(STATIONS - 1 - j).start()
-    for i in reversed(range(STATIONS - CHUNKS)):
-        weight_cross(i).start()
+        if j < STATIONS - early:
+            weight_cross(core, STATIONS - 1 - j).start()
     mine = columns(core)
 
     @pl.when(is_one)
@@ -166,7 +171,9 @@
     for i in reversed(range(STATIONS)):
         weight_copies[i].wait()
         at[core, i] = av[i].T
-        if i == STATIONS // 2:
+        if i < early:
+            weight_cross(core, i).start()
+        if i == early:
             begin(1)
             share_sources(1)
     begin(2)
@@ -174,14 +181,14 @@
 
     rate_cross(1 - core).wait_recv()
 
-    def receive_weights(i):
-        weight_cross(i).wait_recv()
-        at[1 - core, i] = aw[i].T
+    for i in reversed(range(early, STATIONS)):
+        weight_cross(1 - core, i).wait_recv()
+        at[1 - core, i] = aw[i - early].T
 
     @pl.when(jnp.logical_not(first_chip))
     def _():
-        for i in reversed(range(STATIONS)):
-            receive_weights(i)
+        for i in reversed(range(early)):
+            weight_cross(1 - core, i).wait_recv()
 
     def prepare(j):
         @pl.when(jnp.logical_not(first_chip))
@@ -193,10 +200,11 @@
                 halo_copy(j, 0, p).start()
                 halo_copy(j, 1, p).start()
 
-    def arrive(j, p, i):
-        @pl.when(jnp.logical_and(jnp.logical_and(j == 0, first_chip), core != p))
-        def _():
-            receive_weights(i)
+    def arrive(first, p, i):
+        if first and i < early:
+            @pl.when(jnp.logical_and(first_chip, core != p))
+            def _():
+                weight_cross(p, i).wait_recv()
 
     def spread_out(value, rates):
         w = value.astype(F32)
@@ -204,36 +212,30 @@
         spread = w[2 * KC:] + w[:-2 * KC] - 2.0 * center
         return (center + rates * spread).astype(BF)
 
-    def diffuse(j, p, i, value):
-        arrive(j, p, i)
+    def diffuse(first, p, i, value):
+        arrive(first, p, i)
         return spread_out(value, cc[p, i:i + 1, :])
 
-    def station(j, p, i, value):
-        return jnp.dot(diffuse(j, p, i, value), at[p, i], preferred_element_type=F32).astype(BF)
-
-    def compute(j):
+    def station(first, p, i, value):
+        return jnp.dot(diffuse(first, p, i, value), at[p, i], preferred_element_type=F32).astype(BF)
+
+    def compute(j, first):
         n = 3 * rows
         step = 2 * KC
         product = None
         for p in range(PIECES):
             halo_copy(j, 0, p).wait_recv()
             halo_copy(j, 1, p).wait_recv()
-            if p == 0:
-                arrive(j, 1, 3)
             update = spread_out(ext[j, :, lanes(p)], cc[1, 3:4, lanes(p)])
             term = jnp.dot(update, at[1, 3, lanes(p), :], preferred_element_type=F32)
             product = term if product is None else product + term
         wa[pl.ds(0, n - step), :] = product.astype(BF)
-        wb[pl.ds(0, n - 2 * step), :] = station(j, 1, 2, wa[pl.ds(0, n - step), :])
-        wa[pl.ds(0, n - 3 * step), :] = station(j, 1, 1, wb[pl.ds(0, n - 2 * step), :])
+        wb[pl.ds(0, n - 2 * step), :] = station(first, 1, 2, wa[pl.ds(0, n - step), :])
+        wa[pl.ds(0, n - 3 * step), :] = station(first, 1, 1, wb[pl.ds(0, n - 2 * step), :])
         n = 2 * rows
-        upper_out = station(j, 1, 0, wa[pl.ds(0, n + step), :])
+        upper_out = station(first, 1, 0, wa[pl.ds(0, n + step), :])
         wb[pl.ds(0, n), :] = upper_out
         ym[1, j] = wb[middle, :]
-
-        @pl.when(is_one)
-        def _():
-            yf[1, j] = ym[1, j]
 
         @pl.when(is_zero)
         def _():
@@ -242,15 +244,13 @@
         source_halo(j, 0).wait_recv()
         source_halo(j, 1).wait_recv()
         value = (upper_out.astype(F32) + sb[j].astype(F32)).astype(BF)
-        wa[pl.ds(0, n - step), :] = station(j, 0, 3, value)
-        wb[pl.ds(0, n - 2 * step), :] = station(j, 0, 2, wa[pl.ds(0, n - step), :])
-
-        @pl.when(j < CHUNKS - 2)
-        def _():
-            prepare(j + 2)
-
-        wa[pl.ds(0, n - 3 * step), :] = station(j, 0, 1, wb[pl.ds(0, n - 2 * step), :])
-        update = diffuse(j, 0, 0, wa[pl.ds(0, n - 3 * step), :])
+        wa[pl.ds(0, n - step), :] = station(first, 0, 3, value)
+        wb[pl.ds(0, n - 2 * step), :] = station(first, 0, 2, wa[pl.ds(0, n - step), :])
+
+        if first:
+            prepare(2)
+        wa[pl.ds(0, n - 3 * step), :] = station(first, 0, 1, wb[pl.ds(0, n - 2 * step), :])
+        update = diffuse(first, 0, 0, wa[pl.ds(0, n - 3 * step), :])
         for p in range(PIECES):
             ym[0, j, everything, lanes(p)] = jnp.dot(
                 update, at[0, 0, :, lanes(p)], preferred_element_type=F32).astype(BF)
@@ -259,9 +259,7 @@
             def _():
                 main_copy(j, p).start()
 
-        @pl.when(is_zero)
-        def _():
-            yf[0, j] = ym[0, j]
+        yf[core, j] = ym[core, j]
 
         @pl.when(is_one)
         def _():
@@ -270,11 +268,13 @@
     prepare(0)
     prepare(1)
 
+    compute(0, True)
+
     def chunk_step(j, carry):
-        compute(j)
+        compute(j, False)
         return carry
 
-    lax.fori_loop(0, CHUNKS, chunk_step, 0)
+    lax.fori_loop(1, CHUNKS, chunk_step, 0)
     for j in range(CHUNKS):
         cross_y(j).wait_recv()
 
@@ -319,7 +319,7 @@
 
     rate_cross(core).wait_send()
     for i in range(STATIONS):
-        weight_cross(i).wait_send()
+        weight_cross(core, i).wait_send()
     for j in range(CHUNKS):
         source_cross_a(j).wait_send()
         for side in (0, 1):
@@ -400,7 +400,7 @@
         out_specs=(vmem, vmem),
         scratch_shapes=[
             pltpu.VMEM((STATIONS, fn, fn), BF),
-            pltpu.VMEM((STATIONS, fn, fn), BF),
+            pltpu.VMEM((STATIONS - STATIONS // 2, fn, fn), BF),
             pltpu.VMEM((2, STATIONS, fn, fn), BF),
             pltpu.VMEM((STATIONS, fn), F32),
             pltpu.VMEM((2, 2 * STATIONS, fn), F32),

time: 75.8 us -> 72 us (0.950)
  Pallas kernels: 75.1 us -> 71.3 us
    pallas_call x1, Pallas kernels: 73.2 us -> 69.4 us  [local(): pl.pallas_call(functools.partial(march_kernel, sizes, lz, fn, count), nam...]
where the time goes in v5:
time: 72 us; the launch traced here: 71.9 us
  Pallas kernels  71.3 us (99%)
    pallas_call x1, Pallas kernels, local(): pl.pallas_call(functools.partial(march_kernel, sizes, lz, fn, count), nam...  69.4 us
    pallas_call x1, Pallas kernels, local(): pl.pallas_call(functools.partial(basis_kernel, lz), name='basis', out_sha...  1.92 us

profile of v5, /device:TPU:32, one launch (start us, length us, event | category | flops | bytes accessed | tf_op | source)
XLA Modules:
  0.0 71.9 jit_solution(6254929076789706355)
XLA Ops:
  0.6 69.4 %march.1 = (bf16[768,384]{1,0:T(8,128)(2,1)S(1)}, f32[48,128]{1,0:T(8,128)S(1)}) custom-call(bf16[4,768,768]{2,1,0:T(8,128)(2,1)} %a_hbm.1, f32[4,768]{1,0:T(4,128)} %c_hbm.1, bf16[768,384]{1,0:T(8,128)(2,1)} %bitcast.3), custom_call_target="tpu_custom_call" | custom-call | tf_op jit(solution)/shard_map/march/pallas_call | solution.py:395
  70.0 1.9 %basis.1 = (bf16[768,384]{1,0:T(8,128)(2,1)}, f32[48,48]{1,0:T(8,128)}) custom-call(bf16[768,384]{1,0:T(8,128)(2,1)S(1)} %get-tuple-element.6.yt, f32[48,128]{1,0:T(8,128)S(1)} %get-tuple-element.7.w_ref), custom_call_target="tpu_custom_call" | custom-call | tf_op jit(solution)/shard_map/basis/pallas_call | solution.py:432

commit v6 on v5

--- a/solution.py
+++ b/solution.py
@@ -76,7 +76,7 @@
 
     def weight_cross(p, i):
         if i >= early:
-            return remote(a_hbm.at[i], aw.at[i - early], wsend.at[i], wrecv.at[i], other)
+            return remote(av.at[i], aw.at[i - early], wsend.at[i], wrecv.at[i], other)
         return remote(at.at[p, i], at.at[p, i], wsend.at[i], wrecv.at[i], other)
 
     rate_cross = lambda p: remote(cc.at[p], cc.at[p], csend.at[0], crecv.at[0], other)
@@ -128,6 +128,7 @@
             source_cross_b(j).start()
 
         if j < STATIONS - early:
+            weight_copies[STATIONS - 1 - j].wait()
             weight_cross(core, STATIONS - 1 - j).start()
     mine = columns(core)
 
@@ -169,7 +170,8 @@
     cc[core] = jnp.concatenate([cv[...], jnp.zeros_like(cv)], axis=0)
     rate_cross(core).start()
     for i in reversed(range(STATIONS)):
-        weight_copies[i].wait()
+        if i < early:
+            weight_copies[i].wait()
         at[core, i] = av[i].T
         if i < early:
             weight_cross(core, i).start()
@@ -247,9 +249,9 @@
         wa[pl.ds(0, n - step), :] = station(first, 0, 3, value)
         wb[pl.ds(0, n - 2 * step), :] = station(first, 0, 2, wa[pl.ds(0, n - step), :])
 
+        wa[pl.ds(0, n - 3 * step), :] = station(first, 0, 1, wb[pl.ds(0, n - 2 * step), :])
         if first:
             prepare(2)
-        wa[pl.ds(0, n - 3 * step), :] = station(first, 0, 1, wb[pl.ds(0, n - 2 * step), :])
         update = diffuse(first, 0, 0, wa[pl.ds(0, n - 3 * step), :])
         for p in range(PIECES):
             ym[0, j, everything, lanes(p)] = jnp.dot(
@@ -280,18 +282,26 @@
 
     flat = yf[...].reshape(total, fn)
     gram = lax.dot_general(flat, flat, (((1,), (1,)), ((), ())), preferred_element_type=F32)
-    z_of_row = lax.rem(lax.broadcasted_iota(jnp.int32, (total, total), 0), rows) // KC
-    z_of_lane = lax.rem(lax.broadcasted_iota(jnp.int32, (total, total), 1), rows) // KC
-    gram = jnp.where(z_of_row == z_of_lane, gram, 0.0)
-    gram = gram.reshape(2 * CHUNKS, lz, KC, total).sum(1).reshape(K, total)
+    group = (lax.broadcasted_iota(jnp.int32, (KC, total), 1) & (rows - 1)) // KC
+    parts = []
+    for c in range(2 * CHUNKS):
+        part = None
+        for z in range(lz):
+            first = c * rows + z * KC
+            one = jnp.where(group == z, gram[first:first + KC], 0.0)
+            part = one if part is None else part + one
+        parts.append(part)
+    gram = jnp.concatenate(parts, axis=0)
     lane = lax.broadcasted_iota(jnp.int32, (K, 128), 1)
     packed = jnp.zeros((K, 128), F32)
-    for c in range(2 * CHUNKS):
-        pair = gram[:, (c // 2) * 128:(c // 2 + 1) * 128]
-        tile = jnp.where(lane // rows == c % 2, pair, 0.0)
-        for shift in (64, 32, 16, 8):
+    for pair in range(CHUNKS):
+        tile = gram[:, pair * 128:(pair + 1) * 128]
+        for shift in (32, 16, 8):
             tile = tile + pltpu.roll(tile, shift, 1)
-        packed = jnp.where(lane // KC == c, tile, packed)
+        for c in (2 * pair, 2 * pair + 1):
+            end = (c % 2) * rows + rows - KC
+            moved = pltpu.roll(tile, (c * KC - end) % 128, 1)
+            packed = jnp.where(lane // KC == c, moved, packed)
     first, second, third = packed[:16], packed[16:32], packed[32:]
     top = lax.broadcasted_iota(jnp.int32, (16, 128), 1)
     sides = jnp.where(top < 64, pltpu.roll(third, 16, 1), pltpu.roll(second, 48, 1))
@@ -300,7 +310,7 @@
     y_copy = lambda d: remote(gy.at[my], gy.at[my], ysend.at[d - 1], yrecv.at[d - 1], y_peer(d))
     z_copy = lambda d: remote(gz.at[mz], gz.at[mz], zsend.at[d - 1], zrecv.at[d - 1], z_peer(d))
 
-    for d in range(1, ny):
+    for d in sorted(range(1, ny), key=lambda d: -min(d, ny - d)):
         y_copy(d).start()
     yt[...] = flat.T
     for d in range(1, ny):
@@ -309,7 +319,7 @@
     for i in range(1, ny):
         acc = acc + gy[i]
     gz[mz] = acc
-    for d in range(1, nz):
+    for d in sorted(range(1, nz), key=lambda d: -min(d, nz - d)):
         z_copy(d).start()
     for d in range(1, nz):
         z_copy(d).wait_recv()

time: 72 us -> 71.8 us (level)
  no operation moved by 1% of the time
where the time goes in v6:
time: 71.8 us; the launch traced here: 71.7 us
  Pallas kernels  71.1 us (99%)
    pallas_call x1, Pallas kernels, local(): pl.pallas_call(functools.partial(march_kernel, sizes, lz, fn, count), nam...  69.2 us
    pallas_call x1, Pallas kernels, local(): pl.pallas_call(functools.partial(basis_kernel, lz), name='basis', out_sha...  1.92 us

profile of v6, /device:TPU:32, one launch (start us, length us, event | category | flops | bytes accessed | tf_op | source)
XLA Modules:
  0.0 71.7 jit_solution(16175088557371528892)
XLA Ops:
  0.6 69.2 %march.1 = (bf16[768,384]{1,0:T(8,128)(2,1)S(1)}, f32[48,128]{1,0:T(8,128)S(1)}) custom-call(bf16[4,768,768]{2,1,0:T(8,128)(2,1)} %a_hbm.1, f32[4,768]{1,0:T(4,128)} %c_hbm.1, bf16[768,384]{1,0:T(8,128)(2,1)} %bitcast.3), custom_call_target="tpu_custom_call" | custom-call | tf_op jit(solution)/shard_map/march/pallas_call | solution.py:405
  69.8 1.9 %basis.1 = (bf16[768,384]{1,0:T(8,128)(2,1)}, f32[48,48]{1,0:T(8,128)}) custom-call(bf16[768,384]{1,0:T(8,128)(2,1)S(1)} %get-tuple-element.6.yt, f32[48,128]{1,0:T(8,128)S(1)} %get-tuple-element.7.w_ref), custom_call_target="tpu_custom_call" | custom-call | tf_op jit(solution)/shard_map/basis/pallas_call | solution.py:442

commit v7 on v6

--- a/solution.py
+++ b/solution.py
@@ -380,17 +380,15 @@
     block_row = lax.broadcasted_iota(jnp.int32, (rows, lz * K), 0)
     block_lane = lax.broadcasted_iota(jnp.int32, (rows, lz * K), 1)
     same = block_row // KC == block_lane // K
-    out = None
+    blocks = []
     for part in (high, low):
         tiled = lax.dot_general(part, copies, (((0,), (0,)), ((), ())), preferred_element_type=F32)
-        blocks = []
         for c in range(2 * CHUNKS):
             one = tiled[64 + c * KC:64 + (c + 1) * KC]
             blocks.append(jnp.where(same, jnp.concatenate([one] * lz, axis=0), 0.0))
-        block = jnp.concatenate(blocks, axis=0).astype(BF)
-        term = jnp.dot(yt[...], block, preferred_element_type=F32)
-        out = term if out is None else out + term
-    o_ref[...] = out.astype(BF)
+    block = jnp.concatenate(blocks, axis=0).astype(BF)
+    twice = jnp.concatenate([yt[...], yt[...]], axis=1)
+    o_ref[...] = jnp.dot(twice, block, preferred_element_type=F32).astype(BF)
 
 
 def local(sizes, count, inverse_blocks, coupling, sources):

time: 71.8 us -> 71.7 us (level)
  no operation moved by 1% of the time
where the time goes in v7:
time: 71.7 us; the launch traced here: 71.6 us
  Pallas kernels  71 us (99%)
    pallas_call x1, Pallas kernels, local(): pl.pallas_call(functools.partial(march_kernel, sizes, lz, fn, count), nam...  69.2 us
    pallas_call x1, Pallas kernels, local(): pl.pallas_call(functools.partial(basis_kernel, lz), name='basis', out_sha...  1.8 us

profile of v7, /device:TPU:32, one launch (start us, length us, event | category | flops | bytes accessed | tf_op | source)
XLA Modules:
  0.0 71.6 jit_solution(7959547968118629855)
XLA Ops:
  0.6 69.2 %march.1 = (bf16[768,384]{1,0:T(8,128)(2,1)S(1)}, f32[48,128]{1,0:T(8,128)S(1)}) custom-call(bf16[4,768,768]{2,1,0:T(8,128)(2,1)} %a_hbm.1, f32[4,768]{1,0:T(4,128)} %c_hbm.1, bf16[768,384]{1,0:T(8,128)(2,1)} %bitcast.3), custom_call_target="tpu_custom_call" | custom-call | tf_op jit(solution)/shard_map/march/pallas_call | solution.py:403
  69.8 1.8 %basis.1 = (bf16[768,384]{1,0:T(8,128)(2,1)}, f32[48,48]{1,0:T(8,128)}) custom-call(bf16[768,384]{1,0:T(8,128)(2,1)S(1)} %get-tuple-element.6.yt, f32[48,128]{1,0:T(8,128)S(1)} %get-tuple-element.7.w_ref), custom_call_target="tpu_custom_call" | custom-call | tf_op jit(solution)/shard_map/basis/pallas_call | solution.py:440

commit v8 on v7

--- a/solution.py
+++ b/solution.py
@@ -103,19 +103,22 @@
         return remote(sb.at[j, pl.ds(start, half)], sb.at[j, pl.ds(target, half)],
                       bsend.at[j, side], brecv.at[j, side], device)
 
-    source_copy.wait()
     total = 2 * CHUNKS * rows
     pick_row = lax.broadcasted_iota(jnp.int32, (CHUNKS * rows, lz * K), 0)
     pick_lane = lax.broadcasted_iota(jnp.int32, (CHUNKS * rows, lz * K), 1)
     in_chunk = lax.rem(pick_row, rows)
     source_lane = (in_chunk // KC) * K + (pick_row // rows) * KC + lax.rem(in_chunk, KC)
 
-    def columns(h):
-        pick = (pick_lane == source_lane + h * (K // 2)).astype(F32).astype(BF)
+    def selection(h):
+        return (pick_lane == source_lane + h * (K // 2)).astype(F32).astype(BF)
+
+    def columns(pick):
         moved = lax.dot_general(pick, sv[...], (((1,), (1,)), ((), ())), preferred_element_type=F32)
         return moved.astype(BF).reshape(CHUNKS, rows, fn)
 
-    tmp[...] = columns(1 - core)
+    pick_theirs, pick_mine = selection(1 - core), selection(core)
+    source_copy.wait()
+    tmp[...] = columns(pick_theirs)
     pl.semaphore_wait(barrier, ny + nz + 3)
 
     for j in range(CHUNKS):
@@ -130,7 +133,7 @@
         if j < STATIONS - early:
             weight_copies[STATIONS - 1 - j].wait()
             weight_cross(core, STATIONS - 1 - j).start()
-    mine = columns(core)
+    mine = columns(pick_mine)
 
     @pl.when(is_one)
     def _():

time: 71.7 us -> 71.7 us (level)
  no operation moved by 1% of the time
where the time goes in v8:
time: 71.7 us; the launch traced here: 71.6 us
  Pallas kernels  71 us (99%)
    pallas_call x1, Pallas kernels, local(): pl.pallas_call(functools.partial(march_kernel, sizes, lz, fn, count), nam...  69.2 us
    pallas_call x1, Pallas kernels, local(): pl.pallas_call(functools.partial(basis_kernel, lz), name='basis', out_sha...  1.8 us

profile of v8, /device:TPU:32, one launch (start us, length us, event | category | flops | bytes accessed | tf_op | source)
XLA Modules:
  0.0 71.6 jit_solution(5362008947164748669)
XLA Ops:
  0.6 69.2 %march.1 = (bf16[768,384]{1,0:T(8,128)(2,1)S(1)}, f32[48,128]{1,0:T(8,128)S(1)}) custom-call(bf16[4,768,768]{2,1,0:T(8,128)(2,1)} %a_hbm.1, f32[4,768]{1,0:T(4,128)} %c_hbm.1, bf16[768,384]{1,0:T(8,128)(2,1)} %bitcast.3), custom_call_target="tpu_custom_call" | custom-call | tf_op jit(solution)/shard_map/march/pallas_call | solution.py:406
  69.8 1.8 %basis.1 = (bf16[768,384]{1,0:T(8,128)(2,1)}, f32[48,48]{1,0:T(8,128)}) custom-call(bf16[768,384]{1,0:T(8,128)(2,1)S(1)} %get-tuple-element.6.yt, f32[48,128]{1,0:T(8,128)S(1)} %get-tuple-element.7.w_ref), custom_call_target="tpu_custom_call" | custom-call | tf_op jit(solution)/shard_map/basis/pallas_call | solution.py:443

commit v9 on v7

--- a/solution.py
+++ b/solution.py
@@ -312,7 +312,6 @@
 
     for d in sorted(range(1, ny), key=lambda d: -min(d, ny - d)):
         y_copy(d).start()
-    yt[...] = flat.T
     for d in range(1, ny):
         y_copy(d).wait_recv()
     acc = gy[0]
@@ -321,6 +320,7 @@
     gz[mz] = acc
     for d in sorted(range(1, nz), key=lambda d: -min(d, nz - d)):
         z_copy(d).start()
+    yt[...] = flat.T
     for d in range(1, nz):
         z_copy(d).wait_recv()
     acc = gz[0]

time: 71.7 us -> 71.7 us (level)
  no operation moved by 1% of the time
where the time goes in v9:
time: 71.7 us; the launch traced here: 71.6 us
  Pallas kernels  70.9 us (99%)
    pallas_call x1, Pallas kernels, local(): pl.pallas_call(functools.partial(march_kernel, sizes, lz, fn, count), nam...  69.1 us
    pallas_call x1, Pallas kernels, local(): pl.pallas_call(functools.partial(basis_kernel, lz), name='basis', out_sha...  1.8 us

profile of v9, /device:TPU:32, one launch (start us, length us, event | category | flops | bytes accessed | tf_op | source)
XLA Modules:
  0.0 71.6 jit_solution(12807390166673991936)
XLA Ops:
  0.6 69.1 %march.1 = (bf16[768,384]{1,0:T(8,128)(2,1)S(1)}, f32[48,128]{1,0:T(8,128)S(1)}) custom-call(bf16[4,768,768]{2,1,0:T(8,128)(2,1)} %a_hbm.1, f32[4,768]{1,0:T(4,128)} %c_hbm.1, bf16[768,384]{1,0:T(8,128)(2,1)} %bitcast.3), custom_call_target="tpu_custom_call" | custom-call | tf_op jit(solution)/shard_map/march/pallas_call | solution.py:403
  69.8 1.8 %basis.1 = (bf16[768,384]{1,0:T(8,128)(2,1)}, f32[48,48]{1,0:T(8,128)}) custom-call(bf16[768,384]{1,0:T(8,128)(2,1)S(1)} %get-tuple-element.6.yt, f32[48,128]{1,0:T(8,128)S(1)} %get-tuple-element.7.w_ref), custom_call_target="tpu_custom_call" | custom-call | tf_op jit(solution)/shard_map/basis/pallas_call | solution.py:440
